TPU v7x, 512 devices: a whole 4x8x8 slice. The times are simulated.
512 devices in a mesh: mem: 16 (over z_hi, y), reg: 32 (over x, z_lo, core).
Axes of the slice: x: 4, y: 8, z: 8 (z_hi: 2, z_lo: 4; z = z_hi * 4 + z_lo), core: 2. Of those that a mesh axis runs over, the one named last changes fastest.
Arguments:
- ensemble: float32 [256, 131072], P('mem', 'reg'), may hold values from -6 to 6
- obs_pert: float32 [256, 32768], P('mem', 'reg'), may hold values from -45 to 45
- innovation: float32 [32768], P('reg'), may hold values from -6 to 6
- block_list: int32 [512, 8], P(('reg', 'mem')), may hold values from 0 to 255, as said below
- loc_weights: float32 [512, 8, 128], P(('reg', 'mem')), may hold values from 0.05 to 1
Outputs:
- analysis: float32 [256, 131072], P('mem', 'reg')
Inputs may be any that keep to these rules, and one draw needn't show every extreme that they name: `block_list`: each patch lists 8 different blocks. The regions split the patches and the blocks each into equal runs in order; a patch lists only blocks of its own region and of the regions just before and after it, and always the first and the last block of its own region.
All inputs are finite; a program needn't handle non-finite values.
Results may differ from a plain program's by a relative error of at most 0.0003.
Values sent between devices are 32-bit elements; how exact they have to be, the bound alone decides.
No kernel may reach another device: no remote copies, remote signals or barrier semaphores. Data moves between devices by JAX's collectives and lax.ppermute only.
A program may use at most 64 MiB of HBM per device.

v0:
```python
import jax
import jax.numpy as jnp
from jax import lax
from jax.sharding import PartitionSpec as P

NEWTON = 8


def extended(cells, sides, width):
    for axis, dim in sides:
        count = lax.axis_size(axis)
        ends = count - 1
        head = lax.slice_in_dim(cells, 0, width, axis=dim)
        tail = lax.slice_in_dim(cells, cells.shape[dim] - width, cells.shape[dim], axis=dim)
        cells = jnp.concatenate(
            [
                lax.ppermute(tail, axis, [(i, (i + 1) % count) for i in range(ends)]),
                cells,
                lax.ppermute(head, axis, [((i + 1) % count, i) for i in range(ends)]),
            ],
            axis=dim,
        )
    return cells


def batched(first, second, form):
    return jnp.einsum(
        form, first, second, precision=lax.Precision.HIGHEST, preferred_element_type=jnp.float32
    )


def analyse(columns, blocks, innov_blocks, weights):
    members = columns.shape[0]
    ens_mean = jnp.mean(columns, axis=0)
    anomalies = columns - ens_mean[None]
    weighted = blocks * weights[None]
    gram_matrix = batched(weighted, blocks, "kpo,jpo->pkj")
    drive = batched(weighted, innov_blocks, "kpo,po->pk")
    identity = jnp.eye(members, dtype=jnp.float32)
    system = identity[None] + gram_matrix / (members - 1.0)
    trace_sum = jnp.trace(system, axis1=1, axis2=2)
    iterate_y = system / trace_sum[:, None, None]
    iterate_z = identity[None]
    for repeat in range(NEWTON):
        factor = 1.5 * identity[None] - 0.5 * batched(iterate_z, iterate_y, "pij,pjk->pik")
        iterate_y, iterate_z = (
            batched(iterate_y, factor, "pij,pjk->pik"),
            batched(factor, iterate_z, "pij,pjk->pik"),
        )
    root = iterate_z / jnp.sqrt(trace_sum)[:, None, None]
    half_step = batched(root, drive, "pij,pj->pi")
    mean_weights = batched(root, half_step, "pij,pj->pi") / (members - 1.0)
    transform = root + mean_weights[:, :, None]
    return ens_mean[None] + batched(transform, anomalies, "pkj,kps->jps")


def on_device(ensemble, obs_pert, innovation, block_list, loc_weights):
    members = ensemble.shape[0] * lax.axis_size("mem")
    patches_here = block_list.shape[0]
    block_size = loc_weights.shape[2]
    own_obs = obs_pert.shape[1]
    own_blocks = own_obs // block_size
    innov_row = innovation.reshape(1, own_obs)
    whole = lax.all_gather(obs_pert, "mem", axis=0, tiled=True)
    edged, edged_innov = (
        extended(whole, (("reg", 1),), own_obs),
        extended(innov_row, (("reg", 1),), own_obs),
    )
    columns = lax.all_to_all(ensemble, "mem", split_axis=1, concat_axis=0, tiled=True)
    columns = columns.reshape(members, patches_here, columns.shape[1] // patches_here)
    offset = (lax.axis_index("reg") - 1) * own_blocks
    local_blocks = block_list - offset
    edged_blocks = edged.reshape(members, 3 * own_blocks, block_size)
    blocks = jnp.take(edged_blocks, local_blocks, axis=1).reshape(members, patches_here, -1)
    innov_table = edged_innov.reshape(3 * own_blocks, block_size)
    innov_blocks = jnp.take(innov_table, local_blocks, axis=0).reshape(patches_here, -1)
    weights = loc_weights.reshape(patches_here, -1)
    updated = analyse(columns, blocks, innov_blocks, weights).reshape(members, -1)
    return lax.all_to_all(updated, "mem", split_axis=0, concat_axis=1, tiled=True)


def solution(mesh):
    return jax.shard_map(
        on_device,
        mesh=mesh,
        in_specs=(
            P("mem", "reg"),
            P("mem", "reg"),
            P("reg"),
            P(("reg", "mem"), None),
            P(("reg", "mem"), None, None),
        ),
        out_specs=P("mem", "reg"),
        check_vma=False,
    )
```

profile of v0, /device:TPU:10, one launch (start us, length us, event | category | flops | bytes accessed | tf_op | source)
XLA Modules:
  0.0 192.9 jit_solution(6132326483832489951)
XLA Ops:
  6.5 0.0 copy-start.3
  6.5 0.0 all-gather.2.cloned.1.call-start
  6.5 0.7 all-gather.2.cloned.1.call-update
  7.3 1.9 collective-permute-start.2
  9.2 7.3 %collective-permute-start.3 = (f32[1,1024]{1,0:T(1,128)}, f32[1,1024]{1,0:T(1,128)S(1)}, u32[]{:S(2)}, u32[]{:S(2)}) collective-permute-start(f32[1,1024]{1,0:T(1,128)} %bitcast.115), channel_id=1, source_target_pairs={{1,0},{2,1},{3,2},{4,3},{5,4},{6,5},{7,6},{8,7},{9,8},{10,9},{11,1... | collective-permute-start | bytes 12296 | tf_op jit(solution)/shard_map/ppermute | solution.py:19
  16.5 1.7 copy.25
  18.2 15.0 %all-to-all-start = ((f32[16,16,256]{2,0,1:T(8,128)}), f32[16,16,256]{2,0,1:T(8,128)S(1)}, u32[]{:S(2)}, u32[]{:S(2)}) async-start(f32[16,16,256]{2,0,1:T(8,128)} %bitcast.99), calls=%async_computation | async-start | bytes 524288 | tf_op jit(solution)/shard_map/all_to_all | solution.py:69
  33.2 0.7 and_bitcast_fusion
  33.9 0.1 broadcast_bitcast_fusion
  34.0 77.0 %all-gather.2.cloned.1.call-done = f32[256,1024]{1,0:T(8,128)} async-done(((f32[16,1024]{1,0:T(8,128)}), f32[256,1024]{1,0:T(8,128)}) %all-gather.2.cloned.1.call-update) | async-done | bytes 1048592 | tf_op jit(solution)/shard_map/all_gather | solution.py:64
  111.0 1.6 copy.15
  112.5 0.0 copy-start
  112.6 1.9 collective-permute-start
  114.5 6.3 %collective-permute-start.1 = (f32[256,1024]{0,1:T(8,128)S(1)}, f32[256,1024]{0,1:T(8,128)}, u32[]{:S(2)}, u32[]{:S(2)}) collective-permute-start(f32[256,1024]{0,1:T(8,128)S(1)} %copy.15), channel_id=1, source_target_pairs={{1,0},{2,1},{3,2},{4,3},{5,4},{6,5},{7,6},{8,7},{9,8},{10,9},{11,1... | collective-permute-start | bytes 3145736 | tf_op jit(solution)/shard_map/ppermute | solution.py:19
  120.8 0.0 collective-permute-done.2
  120.9 0.0 collective-permute-done.3
  120.9 0.0 copy-done.3
  120.9 0.6 gather_fusion.1
  121.5 0.1 bitcast_select_fusion.1
  121.5 0.0 all-to-all-done
  121.6 20.5 %collective-permute-done = f32[256,1024]{0,1:T(8,128)S(1)} collective-permute-done((f32[256,1024]{0,1:T(8,128)S(1)}, f32[256,1024]{0,1:T(8,128)S(1)}, u32[]{:S(2)}, u32[]{:S(2)}) %collective-permute-start) | collective-permute-done | bytes 1048608 | tf_op jit(solution)/shard_map/ppermute | solution.py:17
  142.1 0.0 copy-done
  142.1 0.0 copy-start.1
  142.1 1.0 copy-done.1
  143.1 0.0 collective-permute-done.1
  143.1 2.1 %pad_maximum_fusion = f32[256,3072]{0,1:T(8,128)S(1)} fusion(f32[256,1024]{0,1:T(8,128)} %collective-permute-done.1, f32[256,1024]{0,1:T(8,128)} %copy-done, f32[256,1024]{0,1:T(8,128)} %copy-done.1), kind=kLoop, calls=%fused_computation.2 | loop fusion | flops 1572864 | bytes 6291456 | tf_op jit(solution)/shard_map/concatenate | solution.py:15
  145.2 2.3 %copy.18 = f32[256,24,128]{2,0,1:T(8,128)} copy(f32[256,24,128]{0,2,1:T(8,128)S(1)} %bitcast.100) | data formatting | bytes 6291456 | tf_op jit(solution)/shard_map/reshape | solution.py:73
  147.5 2.5 %gather_fusion = f32[8,256,128]{2,1,0:T(8,128)S(1)} fusion(f32[256,24,128]{2,0,1:T(8,128)} %copy.18, s32[1024]{0:T(1024)S(1)} %pad_clamp_fusion), kind=kCustom, calls=%fused_computation | custom fusion | bytes 2097184 | tf_op jit(solution)/shard_map/jit(_take)/gather | solution.py:74
  150.0 0.0 copy-start.2
  150.0 0.1 bitcast_select_fusion
  150.2 0.3 copy.20
  150.5 0.3 copy.19
  150.8 0.0 copy-done.2
  150.9 2.7 %select_reduce_fusion = (f32[]{:T(128)}, f32[256,256]{1,0:T(8,128)S(1)}) fusion(f32[256,1024]{0,1:T(8,128)S(1)} %bitcast.104, f32[256,1,1,1,1,1,1024]{0,6,5,4,3,2,1:T(8,128)S(1)} %bitcast.101, f32[1024]{0:T(1024)S(1)} %bitcast.110, pred[1024]{0:T(1024)(128)(4,1)S(1)} %broadcast_bitcast_fusion), kind=kOutput, calls=%fused_computation.38 | convolution fusion | flops 806223872 | bytes 2364420 | tf_op jit(solution)/shard_map/kpo,jpo->pkj/dot_general | solution.py:27
  153.6 1.0 fusion.7
  154.6 1.0 fusion.21
  155.6 0.3 fusion.19
  155.9 0.4 fusion.6
  156.3 0.4 fusion.25
  156.7 0.4 fusion.24
  157.0 0.4 fusion.5
  157.4 0.4 fusion.27
  157.8 0.4 fusion.26
  158.2 0.4 fusion.4
  158.6 0.4 fusion.29
  159.0 0.4 fusion.28
  159.4 0.4 fusion.3
  159.8 0.4 fusion.31
  160.1 0.4 fusion.30
  160.5 0.4 fusion.2
  160.9 0.4 fusion.33
  161.3 0.4 fusion.32
  161.7 0.4 fusion.1
  162.1 0.4 fusion.35
  162.5 0.4 fusion.34
  163.6 0.8 convolution_bitcast_fusion.1
  164.3 0.4 fusion
  164.7 0.4 convolution_divide_fusion
  165.1 0.3 convolution_bitcast_fusion.2
  165.4 0.3 fusion.36
  165.7 0.7 fusion.9
  166.4 18.9 %all_to_all.32 = f32[16,16,256]{2,1,0:T(8,128)S(1)} all-to-all(f32[16,16,256]{2,1,0:T(8,128)S(1)} %bitcast.106), channel_id=1, replica_groups=mesh['mem'=16,'reg'=32] {'mem'}, dimensions={0} | all-to-all | bytes 524288 | tf_op jit(solution)/shard_map/all_to_all | solution.py:79
  185.3 0.7 copy.23
  (6 shorter events, 0.1 us)
Async XLA Ops:
  6.5 114.3 %copy-start.3 = (f32[1024]{0:T(1024)S(1)}, f32[1024]{0:T(1024)}, u32[]{:S(2)}) copy-start(f32[1024]{0:T(1024)} %param.7) | copy-start | bytes 12292
  6.5 104.4 %all-gather.2.cloned.1.call-start = ((), (), s32[]{:S(2)}) async-start(), calls=%async_computation.2 | async-start | bytes 1114112 | tf_op jit(solution)/shard_map/all_gather | solution.py:64
  7.3 113.6 %collective-permute-start.2 = (f32[1,1024]{1,0:T(1,128)}, f32[1,1024]{1,0:T(1,128)S(1)}, u32[]{:S(2)}, u32[]{:S(2)}) collective-permute-start(f32[1,1024]{1,0:T(1,128)} %bitcast.114), channel_id=1, source_target_pairs={{0,1},{1,2},{2,3},{3,4},{4,5},{5,6},{6,7},{7,8},{8,9},{9,10},{10,1... | collective-permute-start | bytes 12296 | tf_op jit(solution)/shard_map/ppermute | solution.py:17
  9.2 111.7 %collective-permute-start.3 = (f32[1,1024]{1,0:T(1,128)}, f32[1,1024]{1,0:T(1,128)S(1)}, u32[]{:S(2)}, u32[]{:S(2)}) collective-permute-start(f32[1,1024]{1,0:T(1,128)} %bitcast.115), channel_id=1, source_target_pairs={{1,0},{2,1},{3,2},{4,3},{5,4},{6,5},{7,6},{8,7},{9,8},{10,9},{11,1... | collective-permute-start | bytes 12296 | tf_op jit(solution)/shard_map/ppermute | solution.py:19
  18.2 103.4 %all-to-all-start = ((f32[16,16,256]{2,0,1:T(8,128)}), f32[16,16,256]{2,0,1:T(8,128)S(1)}, u32[]{:S(2)}, u32[]{:S(2)}) async-start(f32[16,16,256]{2,0,1:T(8,128)} %bitcast.99), calls=%async_computation | async-start | bytes 524288 | tf_op jit(solution)/shard_map/all_to_all | solution.py:69
  112.5 29.6 %copy-start = (f32[256,1024]{0,1:T(8,128)}, f32[256,1024]{0,1:T(8,128)S(1)}, u32[]{:S(2)}) copy-start(f32[256,1024]{0,1:T(8,128)S(1)} %copy.15) | copy-start | bytes 3145732
  112.6 29.6 %collective-permute-start = (f32[256,1024]{0,1:T(8,128)S(1)}, f32[256,1024]{0,1:T(8,128)S(1)}, u32[]{:S(2)}, u32[]{:S(2)}) collective-permute-start(f32[256,1024]{0,1:T(8,128)S(1)} %copy.15), channel_id=1, source_target_pairs={{0,1},{1,2},{2,3},{3,4},{4,5},{5,6},{6,7},{7,8},{8,9},{9,10},{10,1... | collective-permute-start | bytes 3145736 | tf_op jit(solution)/shard_map/ppermute | solution.py:17
  114.5 28.6 %collective-permute-start.1 = (f32[256,1024]{0,1:T(8,128)S(1)}, f32[256,1024]{0,1:T(8,128)}, u32[]{:S(2)}, u32[]{:S(2)}) collective-permute-start(f32[256,1024]{0,1:T(8,128)S(1)} %copy.15), channel_id=1, source_target_pairs={{1,0},{2,1},{3,2},{4,3},{5,4},{6,5},{7,6},{8,7},{9,8},{10,9},{11,1... | collective-permute-start | bytes 3145736 | tf_op jit(solution)/shard_map/ppermute | solution.py:19
  142.1 1.0 copy-start.1
  150.0 0.8 copy-start.2
Sparse Core Ops, SparseCore 0:
  10.5 100.4 all-gather.1
where the time goes:
time: 193 us
  waiting for transfers between devices  98.2 us (51%)
  starting transfers between devices  32.5 us (17%)
  blocking collectives  18.9 us (10%)
  matrix products  14.7 us (8%)
  between operations  14.4 us (7%)
  local copies, waits for them, and re-layouts  11.1 us (6%)
  other arithmetic  3.04 us (2%)
    all_gather x1, waiting for transfers between devices, on_device(): whole = lax.all_gather(obs_pert, 'mem', axis=0, tiled=True)  77 us
    ppermute x2, waiting for transfers between devices, extended(): lax.ppermute(tail, axis, [(i, (i + 1) % count) for i in range(ends)])  20.5 us
    all_to_all x1, blocking collectives, on_device(): lax.all_to_all(updated, 'mem', split_axis=0, concat_axis=1, tiled=True)  18.9 us
    all_to_all x1, starting transfers between devices, on_device(): lax.all_to_all(ensemble, 'mem', split_axis=1, concat_axis=0, tiled=True)  15 us
    dot_general x28, matrix products, batched(): jnp.einsum(form, first, second, precision=lax.Precision.HIGHEST, preferre...  14.7 us
    ppermute x2, starting transfers between devices, extended(): lax.ppermute(head, axis, [((i + 1) % count, i) for i in range(ends)])  13.6 us
  transfers between devices with their start and end apart: 6, of which 2 were waited for; matrix products, arithmetic and copies ran while one was open for 2% of the time, Pallas kernels for 0%

commit v1 on v0

v1 whole, which is shorter than its diff:
```python
import jax
import jax.numpy as jnp
from jax import lax
from jax.experimental import pallas as pl
from jax.experimental.pallas import tpu as pltpu
from jax.sharding import PartitionSpec as P

NEWTON = 8
F32 = jnp.float32
BF16 = jnp.bfloat16
VMEM = pltpu.VMEM


def whole(count):
    return [pl.BlockSpec(memory_space=VMEM)] * count


def pack(ensemble, block_list):
    rows, columns = ensemble.shape
    groups = lax.axis_size("mem")
    width = columns // groups
    halves = width // 128
    depth = halves * rows + 8

    def kernel(ens_ref, list_ref, out_ref):
        tile = jnp.broadcast_to(list_ref[...], (8, 128))
        for patch in range(groups):
            for half in range(halves):
                start = patch * width + half * 128
                out_ref[patch * depth + half * rows : patch * depth + (half + 1) * rows, :] = ens_ref[
                    :, start : start + 128
                ]
            out_ref[patch * depth + halves * rows : (patch + 1) * depth, :] = tile

    listed = jnp.pad(block_list.astype(F32), ((0, 0), (0, 128 - block_list.shape[1])))
    return pl.pallas_call(
        kernel,
        out_shape=jax.ShapeDtypeStruct((groups * depth, 128), F32),
        in_specs=whole(2),
        out_specs=pl.BlockSpec(memory_space=VMEM),
        name="pack",
    )(ensemble, listed)


def select(lists, left, own, right, rows):
    patches = lists.shape[0] - 1
    per_patch = lists.shape[1]
    obs = own.shape[1]
    blocks = obs // 128

    def kernel(lists_ref, left_ref, own_ref, right_ref, out_ref, innov_ref, table, innov_table):
        for side, ref in enumerate((left_ref, own_ref, right_ref)):
            for block in range(blocks):
                at = side * blocks + block
                table[at] = ref[0:rows, block * 128 : (block + 1) * 128]
                innov_table[at] = ref[rows : rows + 1, block * 128 : (block + 1) * 128]
        for patch in range(patches):
            for slot in range(per_patch):
                out_ref[patch * rows : (patch + 1) * rows, slot * 128 : (slot + 1) * 128] = table[
                    lists_ref[patch, slot]
                ]
        for slot in range(per_patch):
            innov_ref[slot : slot + 1, :] = innov_table[lists_ref[patches, slot]]

    return pl.pallas_call(
        kernel,
        out_shape=(
            jax.ShapeDtypeStruct((patches * rows, per_patch * 128), F32),
            jax.ShapeDtypeStruct((per_patch, 128), F32),
        ),
        grid_spec=pltpu.PrefetchScalarGridSpec(
            num_scalar_prefetch=1,
            grid=(),
            in_specs=whole(3),
            out_specs=whole(2),
            scratch_shapes=[
                pltpu.VMEM((3 * blocks, rows, 128), F32),
                pltpu.VMEM((3 * blocks, 1, 128), F32),
            ],
        ),
        name="select",
    )(lists, left, own, right)


def parts(value):
    high = value.astype(BF16)
    return high, (value - high.astype(F32)).astype(BF16)


def product(first, second):
    high1, low1 = first
    high2, low2 = second
    dot = lambda a, b: jnp.dot(a, b, preferred_element_type=F32)
    return dot(high1, high2) + (dot(high1, low2) + dot(low1, high2))


def analyse(obs, innov, weights, packed, rows):
    members, count = obs.shape
    slots = innov.shape[0]
    depth = packed.shape[0] // (members // rows)
    halves = (depth - 8) // rows
    width = halves * 128
    groups = members // rows

    def kernel(obs_ref, innov_ref, weights_ref, packed_ref, out_ref, columns):
        for group in range(groups):
            for half in range(halves):
                columns[group * rows : (group + 1) * rows, half * 128 : (half + 1) * 128] = packed_ref[
                    group * depth + half * rows : group * depth + (half + 1) * rows, :
                ]
        root_weights = jnp.sqrt(weights_ref[...])
        gram_matrix = jnp.zeros((members, members), F32)
        cross = jnp.zeros((members, members), F32)
        drive = jnp.zeros((members, 128), F32)
        contract = lambda a, b: lax.dot_general(
            a, b, (((1,), (1,)), ((), ())), preferred_element_type=F32
        )
        for slot in range(slots):
            scaled = obs_ref[:, slot * 128 : (slot + 1) * 128] * root_weights[slot : slot + 1, :]
            drive += scaled * (root_weights[slot : slot + 1, :] * innov_ref[slot : slot + 1, :])
            high, low = parts(scaled)
            gram_matrix += contract(high, high)
            cross += contract(high, low)
        gram_matrix += cross + cross.T
        drive = jnp.sum(drive, axis=1, keepdims=True)
        identity = (
            lax.broadcasted_iota(jnp.int32, (members, members), 0)
            == lax.broadcasted_iota(jnp.int32, (members, members), 1)
        ).astype(F32)
        system = identity + gram_matrix / (members - 1.0)
        trace_sum = jnp.sum(system * identity, keepdims=True)
        iterate_y = system / trace_sum
        half_three = 1.5 * identity
        factor = half_three - 0.5 * iterate_y
        y_parts = parts(iterate_y)
        z_parts = parts(factor)
        y_parts = parts(product(y_parts, z_parts))
        for repeat in range(1, NEWTON):
            factor = parts(half_three - 0.5 * product(z_parts, y_parts))
            iterate_z = product(factor, z_parts)
            if repeat < NEWTON - 1:
                y_parts = parts(product(y_parts, factor))
                z_parts = parts(iterate_z)
        root = iterate_z / jnp.sqrt(trace_sum)
        half_step = jnp.sum(root * drive, axis=0, keepdims=True)
        mean_weights = jnp.sum(root * half_step, axis=1, keepdims=True) / (members - 1.0)
        ens = columns[...]
        ens_mean = jnp.mean(ens, axis=0, keepdims=True)
        anomalies = ens - ens_mean
        shift = ens_mean + jnp.sum(mean_weights * anomalies, axis=0, keepdims=True)
        out_ref[...] = product(parts(root), parts(anomalies)) + shift

    return pl.pallas_call(
        kernel,
        out_shape=jax.ShapeDtypeStruct((members, width), F32),
        in_specs=whole(4),
        out_specs=pl.BlockSpec(memory_space=VMEM),
        scratch_shapes=[pltpu.VMEM((members, width), F32)],
        name="analyse",
    )(obs, innov, weights, packed)


def on_device(ensemble, obs_pert, innovation, block_list, loc_weights):
    groups = lax.axis_size("mem")
    regions = lax.axis_size("reg")
    rows, own_obs = obs_pert.shape
    weights = loc_weights.reshape(loc_weights.shape[1:])
    slots, block_size = weights.shape
    own_blocks = own_obs // block_size

    packed = lax.all_to_all(pack(ensemble, block_list), "mem", split_axis=0, concat_axis=0, tiled=True)
    table = jnp.concatenate([obs_pert, innovation.reshape(1, own_obs)], axis=0)
    left = lax.ppermute(table, "reg", [(i, i + 1) for i in range(regions - 1)])
    right = lax.ppermute(table, "reg", [(i + 1, i) for i in range(regions - 1)])

    depth = packed.shape[0] // groups
    lists = packed.reshape(groups, depth, 128)[:, depth - 1, :slots].astype(jnp.int32)
    offset = (lax.axis_index("reg") - 1) * own_blocks
    lists = jnp.concatenate([lists, block_list], axis=0) - offset
    chosen, innov = select(lists, left, table, right, rows)
    obs = lax.all_to_all(chosen, "mem", split_axis=0, concat_axis=0, tiled=True)
    updated = analyse(obs, innov, weights, packed, rows)
    sent = lax.all_to_all(updated, "mem", split_axis=0, concat_axis=0, tiled=True)
    return sent.reshape(groups, rows, -1).transpose(1, 0, 2).reshape(rows, -1)


def solution(mesh):
    return jax.shard_map(
        on_device,
        mesh=mesh,
        in_specs=(
            P("mem", "reg"),
            P("mem", "reg"),
            P("reg"),
            P(("reg", "mem"), None),
            P(("reg", "mem"), None, None),
        ),
        out_specs=P("mem", "reg"),
        check_vma=False,
    )
```

time: 193 us -> 106 us (0.55)
  the two profiles are of different devices: /device:TPU:10 before, /device:TPU:8 now
where the time goes in v1:
time: 106 us; the launch traced here: 105 us
  blocking collectives  56.4 us (53%)
  starting transfers between devices  20.5 us (19%)
  Pallas kernels  12.7 us (12%)
  waiting for transfers between devices  10.7 us (10%)
  local copies, waits for them, and re-layouts  3.28 us (3%)
  other arithmetic  1.28 us (1%)
    all_to_all x1, blocking collectives, on_device(): obs = lax.all_to_all(chosen, 'mem', split_axis=0, concat_axis=0, tiled=True)  36.6 us
    all_to_all x1, blocking collectives, on_device(): lax.all_to_all(updated, 'mem', split_axis=0, concat_axis=0, tiled=True)  19.8 us
    all_to_all x1, starting transfers between devices, on_device(): lax.all_to_all(pack(ensemble, block_list), 'mem', split_axis=0, concat_ax...  16.1 us
    all_to_all x1, waiting for transfers between devices, on_device(): lax.all_to_all(pack(ensemble, block_list), 'mem', split_axis=0, concat_ax...  10.7 us
    pallas_call x1, Pallas kernels, analyse(): pl.pallas_call(kernel, out_shape=jax.ShapeDtypeStruct((members, width), F...  8.06 us
    ppermute x1, starting transfers between devices, on_device(): left = lax.ppermute(table, 'reg', [(i, i + 1) for i in range(regions - 1)])  3.04 us
    pallas_call x1, Pallas kernels, select(): pl.pallas_call(kernel, out_shape=(jax.ShapeDtypeStruct((patches * rows, p...  2.93 us
  transfers between devices with their start and end apart: 3, of which 1 were waited for; matrix products, arithmetic and copies ran while one was open for 1% of the time, Pallas kernels for 0%

profile of v1, /device:TPU:8, one launch (start us, length us, event | category | flops | bytes accessed | tf_op | source)
XLA Modules:
  0.0 104.9 jit_solution(13377836762709423187)
XLA Ops:
  0.0 0.7 convert_element_type.11
  0.7 0.5 pad.4.list_ref
  1.2 1.7 %pack.1 = f32[640,128]{1,0:T(8,128)} custom-call(f32[16,4096]{1,0:T(8,128)} %ens_ref.1, f32[1,128]{1,0:T(1,128)} %pad.4.list_ref), custom_call_target="tpu_custom_call" | custom-call | tf_op jit(solution)/shard_map/pack/pallas_call | solution.py:36
  2.9 0.0 copy-start.4
  2.9 0.0 copy-start.5
  2.9 16.1 %all-to-all-start = ((f32[16,40,128]{2,1,0:T(8,128)}), f32[16,40,128]{2,1,0:T(8,128)S(1)}, u32[]{:S(2)}, u32[]{:S(2)}) async-start(f32[16,40,128]{2,1,0:T(8,128)} %bitcast.14), calls=%async_computation | async-start | bytes 655360 | tf_op jit(solution)/shard_map/all_to_all | solution.py:171
  19.0 0.0 copy-done.4
  19.0 0.0 copy-done.5
  19.0 0.0 copy-start.1
  19.1 1.3 %collective-permute-start.1 = (f32[17,1024]{1,0:T(8,128)S(1)}, f32[17,1024]{1,0:T(8,128)S(1)}, u32[]{:S(2)}, u32[]{:S(2)}) collective-permute-start(f32[17,1024]{1,0:T(8,128)S(1)} %pad_maximum_fusion.own_ref), channel_id=1, source_target_pairs={{1,0},{2,1},{3,2},{4,3},{5,4},{6,5},{7,6},{8,7},{9,8},{10,9},{11,1... | collective-permute-start | bytes 208904 | tf_op jit(solution)/shard_map/ppermute | solution.py:174
  20.4 3.0 %collective-permute-start = (f32[17,1024]{1,0:T(8,128)S(1)}, f32[17,1024]{1,0:T(8,128)S(1)}, u32[]{:S(2)}, u32[]{:S(2)}) collective-permute-start(f32[17,1024]{1,0:T(8,128)S(1)} %pad_maximum_fusion.own_ref), channel_id=1, source_target_pairs={{0,1},{1,2},{2,3},{3,4},{4,5},{5,6},{6,7},{7,8},{8,9},{9,10},{10,1... | collective-permute-start | bytes 208904 | tf_op jit(solution)/shard_map/ppermute | solution.py:173
  23.4 10.7 %all-to-all-done = f32[16,40,128]{2,1,0:T(8,128)S(1)} async-done(((f32[16,40,128]{2,1,0:T(8,128)}), f32[16,40,128]{2,1,0:T(8,128)S(1)}, u32[]{:S(2)}, u32[]{:S(2)}) %all-to-all-start) | async-done | bytes 327712 | tf_op jit(solution)/shard_map/all_to_all | solution.py:171
  34.1 0.0 copy-start
  34.1 0.1 copy.17
  34.2 0.0 copy-start.6
  34.2 0.1 copy.15
  34.3 0.6 copy-done.6
  34.9 0.6 add_subtract_fusion.lists_ref
  35.5 0.0 collective-permute-done.1.right_ref
  35.5 0.0 copy-start.2
  35.5 0.0 collective-permute-done.left_ref
  35.5 0.0 copy-done.1
  35.5 0.6 copy-done.2
  36.1 0.0 copy-start.3
  36.1 0.6 copy-done.3
  36.8 2.9 %select.2 = (f32[256,1024]{1,0:T(8,128)}, f32[8,128]{1,0:T(8,128)}) custom-call(s32[17,8]{1,0:T(8,128)} %add_subtract_fusion.lists_ref, f32[17,1024]{1,0:T(8,128)} %copy-done.3, f32[17,1024]{1,0:T(8,128)} %copy-done.1, f32[17,1024]{1,0:T(8,128)} %copy-done.2), custom_call_target="tpu_custom_call" | custom-call | tf_op jit(solution)/shard_map/select/pallas_call | solution.py:65
  39.7 36.6 %all_to_all.31 = f32[16,16,1024]{2,1,0:T(8,128)} all-to-all(f32[16,16,1024]{2,1,0:T(8,128)} %bitcast.16), channel_id=1, replica_groups=mesh['mem'=16,'reg'=32] {'mem'}, dimensions={0} | all-to-all | bytes 2097152 | tf_op jit(solution)/shard_map/all_to_all | solution.py:181
  76.3 0.0 copy-done
  76.3 8.1 %analyse.1 = f32[256,256]{1,0:T(8,128)} custom-call(f32[256,1024]{1,0:T(8,128)} %bitcast.12, f32[8,128]{1,0:T(8,128)} %get-tuple-element.8.innov_ref, f32[8,128]{1,0:T(8,128)} %bitcast.18, f32[640,128]{1,0:T(8,128)} %bitcast.13), custom_call_target="tpu_custom_call" | custom-call | tf_op jit(solution)/shard_map/analyse/pallas_call | solution.py:153
  84.4 19.8 %all_to_all.32 = f32[16,16,256]{2,1,0:T(8,128)S(1)} all-to-all(f32[16,16,256]{2,1,0:T(8,128)} %bitcast.15), channel_id=1, replica_groups=mesh['mem'=16,'reg'=32] {'mem'}, dimensions={0} | all-to-all | bytes 524288 | tf_op jit(solution)/shard_map/all_to_all | solution.py:183
  104.2 0.7 copy.18
  (3 shorter events, 0.0 us)
Async XLA Ops:
  2.9 16.1 %copy-start.4 = (f32[16,1024]{1,0:T(8,128)S(1)}, f32[16,1024]{1,0:T(8,128)}, u32[]{:S(2)}) copy-start(f32[16,1024]{1,0:T(8,128)} %param.6) | copy-start | bytes 196612
  2.9 16.1 %copy-start.5 = (f32[1024]{0:T(1024)S(1)}, f32[1024]{0:T(1024)}, u32[]{:S(2)}) copy-start(f32[1024]{0:T(1024)} %param.7) | copy-start | bytes 12292
  2.9 31.2 %all-to-all-start = ((f32[16,40,128]{2,1,0:T(8,128)}), f32[16,40,128]{2,1,0:T(8,128)S(1)}, u32[]{:S(2)}, u32[]{:S(2)}) async-start(f32[16,40,128]{2,1,0:T(8,128)} %bitcast.14), calls=%async_computation | async-start | bytes 655360 | tf_op jit(solution)/shard_map/all_to_all | solution.py:171
  19.0 16.5 %copy-start.1 = (f32[17,1024]{1,0:T(8,128)}, f32[17,1024]{1,0:T(8,128)S(1)}, u32[]{:S(2)}) copy-start(f32[17,1024]{1,0:T(8,128)S(1)} %pad_maximum_fusion.own_ref) | copy-start | bytes 208900
  19.1 16.4 %collective-permute-start.1 = (f32[17,1024]{1,0:T(8,128)S(1)}, f32[17,1024]{1,0:T(8,128)S(1)}, u32[]{:S(2)}, u32[]{:S(2)}) collective-permute-start(f32[17,1024]{1,0:T(8,128)S(1)} %pad_maximum_fusion.own_ref), channel_id=1, source_target_pairs={{1,0},{2,1},{3,2},{4,3},{5,4},{6,5},{7,6},{8,7},{9,8},{10,9},{11,1... | collective-permute-start | bytes 208904 | tf_op jit(solution)/shard_map/ppermute | solution.py:174
  20.4 15.1 %collective-permute-start = (f32[17,1024]{1,0:T(8,128)S(1)}, f32[17,1024]{1,0:T(8,128)S(1)}, u32[]{:S(2)}, u32[]{:S(2)}) collective-permute-start(f32[17,1024]{1,0:T(8,128)S(1)} %pad_maximum_fusion.own_ref), channel_id=1, source_target_pairs={{0,1},{1,2},{2,3},{3,4},{4,5},{5,6},{6,7},{7,8},{8,9},{9,10},{10,1... | collective-permute-start | bytes 208904 | tf_op jit(solution)/shard_map/ppermute | solution.py:173
  34.1 42.2 %copy-start = (f32[16,40,128]{2,1,0:T(8,128)}, f32[16,40,128]{2,1,0:T(8,128)S(1)}, u32[]{:S(2)}) copy-start(f32[16,40,128]{2,1,0:T(8,128)S(1)} %all-to-all-done) | copy-start | bytes 983044
  34.2 0.7 copy-start.6
  35.5 0.6 copy-start.2
  36.1 0.6 copy-start.3

commit v2 on v1

v2 whole, which is shorter than its diff:
```python
import jax
import jax.numpy as jnp
from jax import lax
from jax.experimental import pallas as pl
from jax.experimental.pallas import tpu as pltpu
from jax.sharding import Mesh
from jax.sharding import PartitionSpec as P

NEWTON = 8
LANES = 128
TILE = 8
HALVES = 2
F32 = jnp.float32
BF16 = jnp.bfloat16
I32 = jnp.int32
MEM = ("half", "ring")


def whole(count):
    return [pl.BlockSpec(memory_space=pltpu.VMEM)] * count


def pack(ensemble, block_list):
    rows, columns = ensemble.shape
    slots = block_list.shape[1]
    groups = lax.axis_size(MEM)
    width = columns // groups
    pieces = width // LANES
    depth = pieces * rows + TILE

    def kernel(ens_ref, list_ref, out_ref, tile_ref):
        tile_ref[...] = jnp.zeros_like(tile_ref)
        tile_ref[0:1, 0:slots] = list_ref[...].astype(F32)
        tile = tile_ref[...]
        for patch in range(groups):
            base = patch * depth
            for piece in range(pieces):
                start = patch * width + piece * LANES
                out_ref[base + piece * rows : base + (piece + 1) * rows, :] = ens_ref[:, start : start + LANES]
            out_ref[base + pieces * rows : base + depth, :] = tile

    return pl.pallas_call(
        kernel,
        out_shape=jax.ShapeDtypeStruct((groups * depth, LANES), F32),
        in_specs=whole(2),
        out_specs=pl.BlockSpec(memory_space=pltpu.VMEM),
        scratch_shapes=[pltpu.VMEM((TILE, LANES), F32)],
        name="pack",
    )(ensemble, block_list)


def select(place, packed, block_list, left, own, right):
    members = own.shape[0] - 1
    obs = own.shape[1]
    blocks = obs // LANES
    slots = block_list.shape[1]
    ring = lax.axis_size("ring")
    groups = HALVES * ring
    depth = packed.shape[0] // groups

    def kernel(
        place_ref, packed_ref, list_ref, left_ref, own_ref, right_ref, out_ref, innov_ref, table, innov_table, lists, wanted, sem
    ):
        half = place_ref[0]
        offset = place_ref[1]
        for source in range(ring):
            at = pl.multiple_of((half * ring + source) * depth + depth - TILE, TILE)
            lists[source : source + 1, :] = packed_ref[pl.ds(at, TILE), :][0:1, :].astype(I32) - offset
        lists[ring : ring + 1, 0:slots] = list_ref[...] - offset
        copy = pltpu.make_async_copy(lists, wanted, sem)
        copy.start()
        for side, ref in enumerate((left_ref, own_ref, right_ref)):
            for block in range(blocks):
                at = side * blocks + block
                table[at] = ref[0:members, block * LANES : (block + 1) * LANES]
                innov_table[at] = ref[members : members + 1, block * LANES : (block + 1) * LANES]
        copy.wait()
        for patch in range(ring):
            for slot in range(slots):
                out_ref[patch * members : (patch + 1) * members, slot * LANES : (slot + 1) * LANES] = table[
                    wanted[patch, slot]
                ]
        for slot in range(slots):
            innov_ref[slot : slot + 1, :] = innov_table[wanted[ring, slot]]

    return pl.pallas_call(
        kernel,
        out_shape=(
            jax.ShapeDtypeStruct((ring * members, slots * LANES), F32),
            jax.ShapeDtypeStruct((slots, LANES), F32),
        ),
        in_specs=[pl.BlockSpec(memory_space=pltpu.SMEM)] + whole(5),
        out_specs=tuple(whole(2)),
        scratch_shapes=[
            pltpu.VMEM((3 * blocks, members, LANES), F32),
            pltpu.VMEM((3 * blocks, 1, LANES), F32),
            pltpu.VMEM((2 * TILE, LANES), I32),
            pltpu.SMEM((2 * TILE, LANES), I32),
            pltpu.SemaphoreType.DMA,
        ],
        name="select",
    )(place, packed, block_list, left, own, right)


def parts(value):
    high = value.astype(BF16)
    return high, (value - high.astype(F32)).astype(BF16)


def product(first, second):
    high1, low1 = first
    high2, low2 = second
    dot = lambda a, b: jnp.dot(a, b, preferred_element_type=F32)
    return dot(high1, high2) + (dot(high1, low2) + dot(low1, high2))


def analyse(place, obs, innov, weights, packed, rows):
    members, count = obs.shape
    slots = innov.shape[0]
    groups = members // rows
    ring = groups // HALVES
    depth = packed.shape[0] // groups
    pieces = (depth - TILE) // rows
    width = pieces * LANES

    def kernel(place_ref, obs_ref, innov_ref, weights_ref, packed_ref, out_ref, columns):
        half = place_ref[0]

        def member_group(chunk):
            return (half ^ (chunk % HALVES)) * ring + chunk // HALVES

        for chunk in range(groups):
            base = member_group(chunk) * depth
            for piece in range(pieces):
                at = pl.multiple_of(base + piece * rows, TILE)
                columns[chunk * rows : (chunk + 1) * rows, piece * LANES : (piece + 1) * LANES] = packed_ref[
                    pl.ds(at, rows), :
                ]
        root_weights = jnp.sqrt(weights_ref[...])
        gram_matrix = jnp.zeros((members, members), F32)
        cross = jnp.zeros((members, members), F32)
        drive = jnp.zeros((members, LANES), F32)
        contract = lambda a, b: lax.dot_general(
            a, b, (((1,), (1,)), ((), ())), preferred_element_type=F32
        )
        for slot in range(slots):
            scaled = obs_ref[:, slot * LANES : (slot + 1) * LANES] * root_weights[slot : slot + 1, :]
            drive += scaled * (root_weights[slot : slot + 1, :] * innov_ref[slot : slot + 1, :])
            high, low = parts(scaled)
            gram_matrix += contract(high, high)
            cross += contract(high, low)
        gram_matrix += cross + cross.T
        drive = jnp.sum(drive, axis=1, keepdims=True)
        identity = (
            lax.broadcasted_iota(I32, (members, members), 0) == lax.broadcasted_iota(I32, (members, members), 1)
        ).astype(F32)
        system = identity + gram_matrix / (members - 1.0)
        trace_sum = jnp.sum(system * identity, keepdims=True)
        iterate_y = system / trace_sum
        half_three = 1.5 * identity
        factor = half_three - 0.5 * iterate_y
        y_parts = parts(iterate_y)
        z_parts = parts(factor)
        y_parts = parts(product(y_parts, z_parts))
        for repeat in range(1, NEWTON):
            factor = parts(half_three - 0.5 * product(z_parts, y_parts))
            iterate_z = product(factor, z_parts)
            if repeat < NEWTON - 1:
                y_parts = parts(product(y_parts, factor))
                z_parts = parts(iterate_z)
        root = iterate_z / jnp.sqrt(trace_sum)
        half_step = jnp.sum(root * drive, axis=0, keepdims=True)
        mean_weights = jnp.sum(root * half_step, axis=1, keepdims=True) / (members - 1.0)
        ens = columns[...]
        ens_mean = jnp.mean(ens, axis=0, keepdims=True)
        anomalies = ens - ens_mean
        shift = ens_mean + jnp.sum(mean_weights * anomalies, axis=0, keepdims=True)
        updated = product(parts(root), parts(anomalies)) + shift
        for chunk in range(groups):
            at = pl.multiple_of(member_group(chunk) * rows, TILE)
            out_ref[pl.ds(at, rows), :] = updated[chunk * rows : (chunk + 1) * rows, :]

    return pl.pallas_call(
        kernel,
        out_shape=jax.ShapeDtypeStruct((members, width), F32),
        in_specs=[pl.BlockSpec(memory_space=pltpu.SMEM)] + whole(4),
        out_specs=pl.BlockSpec(memory_space=pltpu.VMEM),
        scratch_shapes=[pltpu.VMEM((members, width), F32)],
        name="analyse",
    )(place, obs, innov, weights, packed)


def on_device(ensemble, obs_pert, innovation, block_list, loc_weights):
    regions = lax.axis_size("reg")
    rows, own_obs = obs_pert.shape
    weights = loc_weights.reshape(loc_weights.shape[1:])
    block_size = weights.shape[1]
    own_blocks = own_obs // block_size
    place = jnp.stack([lax.axis_index("half"), (lax.axis_index("reg") - 1) * own_blocks]).astype(I32)

    partner = lax.ppermute(obs_pert, "half", [(0, 1), (1, 0)])
    packed = lax.all_to_all(pack(ensemble, block_list), MEM, split_axis=0, concat_axis=0, tiled=True)
    table = jnp.concatenate([obs_pert, partner, innovation.reshape(1, own_obs)], axis=0)
    left = lax.ppermute(table, "reg", [(i, i + 1) for i in range(regions - 1)])
    right = lax.ppermute(table, "reg", [(i + 1, i) for i in range(regions - 1)])
    chosen, innov = select(place, packed, block_list, left, table, right)
    obs = lax.all_to_all(chosen, "ring", split_axis=0, concat_axis=0, tiled=True)
    updated = analyse(place, obs, innov, weights, packed, rows)
    sent = lax.all_to_all(updated, MEM, split_axis=0, concat_axis=0, tiled=True)
    return sent.reshape(sent.shape[0] // rows, rows, -1).transpose(1, 0, 2).reshape(rows, -1)


def solution(mesh):
    groups, regions = (mesh.shape[name] for name in ("mem", "reg"))
    fine = Mesh(mesh.devices.reshape(HALVES, groups // HALVES, regions), MEM + ("reg",))
    return jax.shard_map(
        on_device,
        mesh=fine,
        in_specs=(
            P(MEM, "reg"),
            P(MEM, "reg"),
            P("reg"),
            P(("reg",) + MEM, None),
            P(("reg",) + MEM, None, None),
        ),
        out_specs=P(MEM, "reg"),
        check_vma=False,
    )
```

time: 106 us -> 108 us (1.019)
  the two profiles are of different devices: /device:TPU:8 before, /device:TPU:10 now
where the time goes in v2:
time: 108 us; the launch traced here: 107 us
  blocking collectives  47.4 us (44%)
  starting transfers between devices  30.2 us (28%)
  waiting for transfers between devices  14.4 us (13%)
  Pallas kernels  12.7 us (12%)
  local copies, waits for them, and re-layouts  1.49 us (1%)
    all_to_all x1, blocking collectives, on_device(): lax.all_to_all(chosen, 'ring', split_axis=0, concat_axis=0, tiled=True)  29.6 us
    all_to_all x1, blocking collectives, on_device(): sent = lax.all_to_all(updated, MEM, split_axis=0, concat_axis=0, tiled=True)  17.8 us
    all_to_all x1, starting transfers between devices, on_device(): lax.all_to_all(pack(ensemble, block_list), MEM, split_axis=0, concat_axis...  16.1 us
    pallas_call x1, Pallas kernels, analyse(): pl.pallas_call(kernel, out_shape=jax.ShapeDtypeStruct((members, width), F...  8.07 us
    ppermute x1, waiting for transfers between devices, on_device(): partner = lax.ppermute(obs_pert, 'half', [(0, 1), (1, 0)])  7.63 us
    ppermute x1, starting transfers between devices, on_device(): partner = lax.ppermute(obs_pert, 'half', [(0, 1), (1, 0)])  7.28 us
    ppermute x1, starting transfers between devices, on_device(): right = lax.ppermute(table, 'reg', [(i + 1, i) for i in range(regions - 1)])  4.82 us
    ppermute x1, waiting for transfers between devices, on_device(): left = lax.ppermute(table, 'reg', [(i, i + 1) for i in range(regions - 1)])  4.77 us
  transfers between devices with their start and end apart: 4, of which 3 were waited for; matrix products, arithmetic and copies ran while one was open for 1% of the time, Pallas kernels for 0%

profile of v2, /device:TPU:10, one launch (start us, length us, event | category | flops | bytes accessed | tf_op | source)
XLA Modules:
  0.0 106.9 jit_solution(18351005880040286937)
XLA Ops:
  0.0 1.7 %pack.1 = f32[640,128]{1,0:T(8,128)} custom-call(f32[16,4096]{1,0:T(8,128)} %ens_ref.1, s32[1,8]{1,0:T(1,128)} %list_ref.3), custom_call_target="tpu_custom_call" | custom-call | tf_op jit(solution)/shard_map/pack/pallas_call | solution.py:42
  1.7 0.0 copy-start.4
  1.7 0.0 copy-start.5
  1.7 16.1 %all-to-all-start = ((f32[16,40,128]{2,1,0:T(8,128)}), f32[16,40,128]{2,1,0:T(8,128)S(1)}, u32[]{:S(2)}, u32[]{:S(2)}) async-start(f32[16,40,128]{2,1,0:T(8,128)} %bitcast.15), calls=%async_computation | async-start | bytes 655360 | tf_op jit(solution)/shard_map/all_to_all | solution.py:202
  17.8 0.0 copy-done.4
  17.8 7.3 %collective-permute-start = (f32[16,1024]{1,0:T(8,128)S(1)}, f32[16,1024]{1,0:T(8,128)S(1)}, u32[]{:S(2)}, u32[]{:S(2)}) collective-permute-start(f32[16,1024]{1,0:T(8,128)S(1)} %copy-done.4), channel_id=1, source_target_pairs={{0,256},{256,0},{1,257},{257,1},{2,258},{258,2},{3,259},{259,3},{4... | collective-permute-start | bytes 196616 | tf_op jit(solution)/shard_map/ppermute | solution.py:201
  25.1 7.6 %collective-permute-done = f32[16,1024]{1,0:T(8,128)S(1)} collective-permute-done((f32[16,1024]{1,0:T(8,128)S(1)}, f32[16,1024]{1,0:T(8,128)S(1)}, u32[]{:S(2)}, u32[]{:S(2)}) %collective-permute-start) | collective-permute-done | bytes 65568 | tf_op jit(solution)/shard_map/ppermute | solution.py:201
  32.8 0.0 copy-done.5
  32.8 0.0 copy-start.1
  32.8 4.8 %collective-permute-start.2 = (f32[33,1024]{1,0:T(8,128)S(1)}, f32[33,1024]{1,0:T(8,128)S(1)}, u32[]{:S(2)}, u32[]{:S(2)}) collective-permute-start(f32[33,1024]{1,0:T(8,128)S(1)} %pad_maximum_fusion.own_ref), channel_id=1, source_target_pairs={{1,0},{2,1},{3,2},{4,3},{5,4},{6,5},{7,6},{8,7},{9,8},{10,9},{11,1... | collective-permute-start | bytes 405512 | tf_op jit(solution)/shard_map/ppermute | solution.py:205
  37.6 1.9 %collective-permute-start.1 = (f32[33,1024]{1,0:T(8,128)S(1)}, f32[33,1024]{1,0:T(8,128)S(1)}, u32[]{:S(2)}, u32[]{:S(2)}) collective-permute-start(f32[33,1024]{1,0:T(8,128)S(1)} %pad_maximum_fusion.own_ref), channel_id=1, source_target_pairs={{0,1},{1,2},{2,3},{3,4},{4,5},{5,6},{6,7},{7,8},{8,9},{9,10},{10,1... | collective-permute-start | bytes 405512 | tf_op jit(solution)/shard_map/ppermute | solution.py:204
  39.6 0.7 pad_add_fusion.place_ref
  40.2 2.0 %collective-permute-done.2.right_ref = f32[33,1024]{1,0:T(8,128)S(1)} collective-permute-done((f32[33,1024]{1,0:T(8,128)S(1)}, f32[33,1024]{1,0:T(8,128)S(1)}, u32[]{:S(2)}, u32[]{:S(2)}) %collective-permute-start.2) | collective-permute-done | bytes 135200 | tf_op jit(solution)/shard_map/ppermute | solution.py:205
  42.2 0.0 copy-start.2
  42.2 4.8 %collective-permute-done.1.left_ref = f32[33,1024]{1,0:T(8,128)S(1)} collective-permute-done((f32[33,1024]{1,0:T(8,128)S(1)}, f32[33,1024]{1,0:T(8,128)S(1)}, u32[]{:S(2)}, u32[]{:S(2)}) %collective-permute-start.1) | collective-permute-done | bytes 135200 | tf_op jit(solution)/shard_map/ppermute | solution.py:204
  47.0 0.0 copy-start.3
  47.0 0.0 all-to-all-done
  47.0 0.0 copy-start
  47.0 0.0 copy-done.1
  47.0 0.0 copy-done.2
  47.0 0.6 copy-done.3
  47.6 0.1 copy-done
  47.7 2.9 %select.1 = (f32[256,1024]{1,0:T(8,128)}, f32[8,128]{1,0:T(8,128)}) custom-call(s32[2]{0:T(128)} %pad_add_fusion.place_ref, f32[640,128]{1,0:T(8,128)} %bitcast.13, s32[1,8]{1,0:T(1,128)} %list_ref.3, f32[33,1024]{1,0:T(8,128)} %copy-done.3, f32[33,1024]{1,0:T(8,128)} %copy-done.1, f32[33,1024]{1,0:T(8,128)} %copy-done.2), custom_call_target="tpu_custom_call" | custom-call | tf_op jit(solution)/shard_map/select/pallas_call | solution.py:86
  50.7 29.6 %all_to_all.31 = f32[8,32,1024]{2,1,0:T(8,128)} all-to-all(f32[8,32,1024]{2,1,0:T(8,128)} %bitcast.16), channel_id=1, replica_groups=mesh['half'=2,'ring'=8,'reg'=32] {'ring'}, dimensions={0} | all-to-all | bytes 2097152 | tf_op jit(solution)/shard_map/all_to_all | solution.py:207
  80.3 8.1 %analyse.1 = f32[256,256]{1,0:T(8,128)} custom-call(s32[2]{0:T(128)} %pad_add_fusion.place_ref, f32[256,1024]{1,0:T(8,128)} %bitcast.12, f32[8,128]{1,0:T(8,128)} %get-tuple-element.8.innov_ref, f32[8,128]{1,0:T(8,128)} %bitcast.20, f32[640,128]{1,0:T(8,128)} %bitcast.14), custom_call_target="tpu_custom_call" | custom-call | tf_op jit(solution)/shard_map/analyse/pallas_call | solution.py:183
  88.4 17.8 %all_to_all.32 = f32[16,16,256]{2,1,0:T(8,128)S(1)} all-to-all(f32[16,16,256]{2,1,0:T(8,128)} %bitcast.18), channel_id=1, replica_groups=mesh['half'=2,'ring'=8,'reg'=32] {'half','ring'}, dimensions={0} | all-to-all | bytes 524288 | tf_op jit(solution)/shard_map/all_to_all | solution.py:209
  106.2 0.7 copy.7
  (1 shorter events, 0.0 us)
Async XLA Ops:
  1.7 16.1 %copy-start.4 = (f32[16,1024]{1,0:T(8,128)S(1)}, f32[16,1024]{1,0:T(8,128)}, u32[]{:S(2)}) copy-start(f32[16,1024]{1,0:T(8,128)} %param.6) | copy-start | bytes 196612
  1.7 31.1 %copy-start.5 = (f32[1024]{0:T(1024)S(1)}, f32[1024]{0:T(1024)}, u32[]{:S(2)}) copy-start(f32[1024]{0:T(1024)} %param.7) | copy-start | bytes 12292
  1.7 45.3 %all-to-all-start = ((f32[16,40,128]{2,1,0:T(8,128)}), f32[16,40,128]{2,1,0:T(8,128)S(1)}, u32[]{:S(2)}, u32[]{:S(2)}) async-start(f32[16,40,128]{2,1,0:T(8,128)} %bitcast.15), calls=%async_computation | async-start | bytes 655360 | tf_op jit(solution)/shard_map/all_to_all | solution.py:202
  17.8 14.9 %collective-permute-start = (f32[16,1024]{1,0:T(8,128)S(1)}, f32[16,1024]{1,0:T(8,128)S(1)}, u32[]{:S(2)}, u32[]{:S(2)}) collective-permute-start(f32[16,1024]{1,0:T(8,128)S(1)} %copy-done.4), channel_id=1, source_target_pairs={{0,256},{256,0},{1,257},{257,1},{2,258},{258,2},{3,259},{259,3},{4... | collective-permute-start | bytes 196616 | tf_op jit(solution)/shard_map/ppermute | solution.py:201
  32.8 14.2 %copy-start.1 = (f32[33,1024]{1,0:T(8,128)}, f32[33,1024]{1,0:T(8,128)S(1)}, u32[]{:S(2)}) copy-start(f32[33,1024]{1,0:T(8,128)S(1)} %pad_maximum_fusion.own_ref) | copy-start | bytes 405508
  32.8 9.4 %collective-permute-start.2 = (f32[33,1024]{1,0:T(8,128)S(1)}, f32[33,1024]{1,0:T(8,128)S(1)}, u32[]{:S(2)}, u32[]{:S(2)}) collective-permute-start(f32[33,1024]{1,0:T(8,128)S(1)} %pad_maximum_fusion.own_ref), channel_id=1, source_target_pairs={{1,0},{2,1},{3,2},{4,3},{5,4},{6,5},{7,6},{8,7},{9,8},{10,9},{11,1... | collective-permute-start | bytes 405512 | tf_op jit(solution)/shard_map/ppermute | solution.py:205
  37.6 9.3 %collective-permute-start.1 = (f32[33,1024]{1,0:T(8,128)S(1)}, f32[33,1024]{1,0:T(8,128)S(1)}, u32[]{:S(2)}, u32[]{:S(2)}) collective-permute-start(f32[33,1024]{1,0:T(8,128)S(1)} %pad_maximum_fusion.own_ref), channel_id=1, source_target_pairs={{0,1},{1,2},{2,3},{3,4},{4,5},{5,6},{6,7},{7,8},{8,9},{9,10},{10,1... | collective-permute-start | bytes 405512 | tf_op jit(solution)/shard_map/ppermute | solution.py:204
  42.2 4.8 %copy-start.2 = (f32[33,1024]{1,0:T(8,128)}, f32[33,1024]{1,0:T(8,128)S(1)}, u32[]{:S(2)}) copy-start(f32[33,1024]{1,0:T(8,128)S(1)} %collective-permute-done.2.right_ref) | copy-start | bytes 405508
  47.0 0.7 copy-start.3
  47.0 0.8 copy-start

commit v3 on v2

--- a/solution.py
+++ b/solution.py
@@ -5,6 +5,7 @@
 from jax.experimental.pallas import tpu as pltpu
 from jax.sharding import Mesh
 from jax.sharding import PartitionSpec as P
+
 
 NEWTON = 8
 LANES = 128
@@ -18,6 +19,10 @@
 
 def whole(count):
     return [pl.BlockSpec(memory_space=pltpu.VMEM)] * count
+
+
+def near(*arrays):
+    return [pltpu.with_memory_space_constraint(value, pltpu.VMEM) for value in arrays]
 
 
 def pack(ensemble, block_list):
@@ -41,7 +46,7 @@
 
     return pl.pallas_call(
         kernel,
-        out_shape=jax.ShapeDtypeStruct((groups * depth, LANES), F32),
+        out_shape=pltpu.VMEM((groups * depth, LANES), F32),
         in_specs=whole(2),
         out_specs=pl.BlockSpec(memory_space=pltpu.VMEM),
         scratch_shapes=[pltpu.VMEM((TILE, LANES), F32)],
@@ -49,7 +54,7 @@
     )(ensemble, block_list)
 
 
-def select(place, packed, block_list, left, own, right):
+def select(packed, block_list, left, own, right):
     members = own.shape[0] - 1
     obs = own.shape[1]
     blocks = obs // LANES
@@ -59,10 +64,10 @@
     depth = packed.shape[0] // groups
 
     def kernel(
-        place_ref, packed_ref, list_ref, left_ref, own_ref, right_ref, out_ref, innov_ref, table, innov_table, lists, wanted, sem
+        packed_ref, list_ref, left_ref, own_ref, right_ref, out_ref, innov_ref, table, innov_table, lists, wanted, sem
     ):
-        half = place_ref[0]
-        offset = place_ref[1]
+        half = lax.axis_index("half")
+        offset = (lax.axis_index("reg") - 1) * blocks
         for source in range(ring):
             at = pl.multiple_of((half * ring + source) * depth + depth - TILE, TILE)
             lists[source : source + 1, :] = packed_ref[pl.ds(at, TILE), :][0:1, :].astype(I32) - offset
@@ -86,10 +91,10 @@
     return pl.pallas_call(
         kernel,
         out_shape=(
-            jax.ShapeDtypeStruct((ring * members, slots * LANES), F32),
-            jax.ShapeDtypeStruct((slots, LANES), F32),
+            pltpu.VMEM((ring * members, slots * LANES), F32),
+            pltpu.VMEM((slots, LANES), F32),
         ),
-        in_specs=[pl.BlockSpec(memory_space=pltpu.SMEM)] + whole(5),
+        in_specs=whole(5),
         out_specs=tuple(whole(2)),
         scratch_shapes=[
             pltpu.VMEM((3 * blocks, members, LANES), F32),
@@ -99,7 +104,7 @@
             pltpu.SemaphoreType.DMA,
         ],
         name="select",
-    )(place, packed, block_list, left, own, right)
+    )(*near(packed), block_list, *near(left, own, right))
 
 
 def parts(value):
@@ -114,8 +119,8 @@
     return dot(high1, high2) + (dot(high1, low2) + dot(low1, high2))
 
 
-def analyse(place, obs, innov, weights, packed, rows):
-    members, count = obs.shape
+def analyse(obs, innov, weights, packed, rows):
+    members, _ = obs.shape
     slots = innov.shape[0]
     groups = members // rows
     ring = groups // HALVES
@@ -123,8 +128,8 @@
     pieces = (depth - TILE) // rows
     width = pieces * LANES
 
-    def kernel(place_ref, obs_ref, innov_ref, weights_ref, packed_ref, out_ref, columns):
-        half = place_ref[0]
+    def kernel(obs_ref, innov_ref, weights_ref, packed_ref, out_ref, columns):
+        half = lax.axis_index("half")
 
         def member_group(chunk):
             return (half ^ (chunk % HALVES)) * ring + chunk // HALVES
@@ -182,30 +187,28 @@
 
     return pl.pallas_call(
         kernel,
-        out_shape=jax.ShapeDtypeStruct((members, width), F32),
-        in_specs=[pl.BlockSpec(memory_space=pltpu.SMEM)] + whole(4),
+        out_shape=pltpu.VMEM((members, width), F32),
+        in_specs=whole(4),
         out_specs=pl.BlockSpec(memory_space=pltpu.VMEM),
         scratch_shapes=[pltpu.VMEM((members, width), F32)],
         name="analyse",
-    )(place, obs, innov, weights, packed)
+    )(*near(obs, innov), weights, *near(packed))
 
 
 def on_device(ensemble, obs_pert, innovation, block_list, loc_weights):
     regions = lax.axis_size("reg")
     rows, own_obs = obs_pert.shape
     weights = loc_weights.reshape(loc_weights.shape[1:])
-    block_size = weights.shape[1]
-    own_blocks = own_obs // block_size
-    place = jnp.stack([lax.axis_index("half"), (lax.axis_index("reg") - 1) * own_blocks]).astype(I32)
 
     partner = lax.ppermute(obs_pert, "half", [(0, 1), (1, 0)])
-    packed = lax.all_to_all(pack(ensemble, block_list), MEM, split_axis=0, concat_axis=0, tiled=True)
+    packed = pack(ensemble, block_list)
+    packed = lax.all_to_all(packed, MEM, split_axis=0, concat_axis=0, tiled=True)
     table = jnp.concatenate([obs_pert, partner, innovation.reshape(1, own_obs)], axis=0)
     left = lax.ppermute(table, "reg", [(i, i + 1) for i in range(regions - 1)])
     right = lax.ppermute(table, "reg", [(i + 1, i) for i in range(regions - 1)])
-    chosen, innov = select(place, packed, block_list, left, table, right)
+    chosen, innov = select(packed, block_list, left, table, right)
     obs = lax.all_to_all(chosen, "ring", split_axis=0, concat_axis=0, tiled=True)
-    updated = analyse(place, obs, innov, weights, packed, rows)
+    updated = analyse(obs, innov, weights, packed, rows)
     sent = lax.all_to_all(updated, MEM, split_axis=0, concat_axis=0, tiled=True)
     return sent.reshape(sent.shape[0] // rows, rows, -1).transpose(1, 0, 2).reshape(rows, -1)
 

time: 108 us -> 103 us (0.954)
  the two profiles are of different devices: /device:TPU:10 before, /device:TPU:14 now
where the time goes in v3:
time: 103 us; the launch traced here: 102 us
  blocking collectives  46 us (45%)
  starting transfers between devices  30.5 us (30%)
  waiting for transfers between devices  15 us (15%)
  Pallas kernels  9.87 us (10%)
    all_to_all x1, blocking collectives, on_device(): lax.all_to_all(chosen, 'ring', split_axis=0, concat_axis=0, tiled=True)  29.1 us
    all_to_all x1, blocking collectives, on_device(): sent = lax.all_to_all(updated, MEM, split_axis=0, concat_axis=0, tiled=True)  16.9 us
    all_to_all x1, starting transfers between devices, on_device(): lax.all_to_all(packed, MEM, split_axis=0, concat_axis=0, tiled=True)  16.1 us
    ppermute x1, waiting for transfers between devices, on_device(): partner = lax.ppermute(obs_pert, 'half', [(0, 1), (1, 0)])  7.63 us
    ppermute x1, starting transfers between devices, on_device(): partner = lax.ppermute(obs_pert, 'half', [(0, 1), (1, 0)])  7.28 us
    pallas_call x1, Pallas kernels, analyse(): pl.pallas_call(kernel, out_shape=pltpu.VMEM((members, width), F32), in_sp...  6.74 us
    ppermute x1, starting transfers between devices, on_device(): right = lax.ppermute(table, 'reg', [(i + 1, i) for i in range(regions - 1)])  5.11 us
    ppermute x1, waiting for transfers between devices, on_device(): left = lax.ppermute(table, 'reg', [(i, i + 1) for i in range(regions - 1)])  5.08 us
  transfers between devices with their start and end apart: 4, of which 3 were waited for; matrix products, arithmetic and copies ran while one was open for 0% of the time, Pallas kernels for 0%

profile of v3, /device:TPU:14, one launch (start us, length us, event | category | flops | bytes accessed | tf_op | source)
XLA Modules:
  0.0 102.2 jit_solution(519594614677535835)
XLA Ops:
  0.0 1.7 %pack.1 = f32[640,128]{1,0:T(8,128)} custom-call(f32[16,4096]{1,0:T(8,128)} %ens_ref.1, s32[1,8]{1,0:T(1,128)} %list_ref.3), custom_call_target="tpu_custom_call" | custom-call | tf_op jit(solution)/shard_map/pack/pallas_call | solution.py:47
  1.7 0.0 copy-start
  1.7 0.0 copy-start.1
  1.7 16.1 %all-to-all-start = ((f32[16,40,128]{2,1,0:T(8,128)}), f32[16,40,128]{2,1,0:T(8,128)S(1)}, u32[]{:S(2)}, u32[]{:S(2)}) async-start(f32[16,40,128]{2,1,0:T(8,128)} %bitcast), calls=%async_computation | async-start | bytes 655360 | tf_op jit(solution)/shard_map/all_to_all | solution.py:205
  17.8 0.0 copy-done
  17.8 7.3 %collective-permute-start = (f32[16,1024]{1,0:T(8,128)S(1)}, f32[16,1024]{1,0:T(8,128)S(1)}, u32[]{:S(2)}, u32[]{:S(2)}) collective-permute-start(f32[16,1024]{1,0:T(8,128)S(1)} %copy-done), channel_id=1, source_target_pairs={{0,256},{256,0},{1,257},{257,1},{2,258},{258,2},{3,259},{259,3},{4... | collective-permute-start | bytes 196616 | tf_op jit(solution)/shard_map/ppermute | solution.py:203
  25.1 7.6 %collective-permute-done = f32[16,1024]{1,0:T(8,128)S(1)} collective-permute-done((f32[16,1024]{1,0:T(8,128)S(1)}, f32[16,1024]{1,0:T(8,128)S(1)}, u32[]{:S(2)}, u32[]{:S(2)}) %collective-permute-start) | collective-permute-done | bytes 65568 | tf_op jit(solution)/shard_map/ppermute | solution.py:203
  32.8 0.0 copy-done.1
  32.8 5.1 %collective-permute-start.2 = (f32[33,1024]{1,0:T(8,128)S(1)}, f32[33,1024]{1,0:T(8,128)S(1)}, u32[]{:S(2)}, u32[]{:S(2)}) collective-permute-start(f32[33,1024]{1,0:T(8,128)S(1)} %pad_maximum_fusion.own_ref), channel_id=1, source_target_pairs={{1,0},{2,1},{3,2},{4,3},{5,4},{6,5},{7,6},{8,7},{9,8},{10,9},{11,1... | collective-permute-start | bytes 405512 | tf_op jit(solution)/shard_map/ppermute | solution.py:208
  37.9 1.9 %collective-permute-start.1 = (f32[33,1024]{1,0:T(8,128)S(1)}, f32[33,1024]{1,0:T(8,128)S(1)}, u32[]{:S(2)}, u32[]{:S(2)}) collective-permute-start(f32[33,1024]{1,0:T(8,128)S(1)} %pad_maximum_fusion.own_ref), channel_id=1, source_target_pairs={{0,1},{1,2},{2,3},{3,4},{4,5},{5,6},{6,7},{7,8},{8,9},{9,10},{10,1... | collective-permute-start | bytes 405512 | tf_op jit(solution)/shard_map/ppermute | solution.py:207
  39.8 2.3 %collective-permute-done.2.right_ref = f32[33,1024]{1,0:T(8,128)S(1)} collective-permute-done((f32[33,1024]{1,0:T(8,128)S(1)}, f32[33,1024]{1,0:T(8,128)S(1)}, u32[]{:S(2)}, u32[]{:S(2)}) %collective-permute-start.2) | collective-permute-done | bytes 135200 | tf_op jit(solution)/shard_map/ppermute | solution.py:208
  42.2 5.1 %collective-permute-done.1.left_ref = f32[33,1024]{1,0:T(8,128)S(1)} collective-permute-done((f32[33,1024]{1,0:T(8,128)S(1)}, f32[33,1024]{1,0:T(8,128)S(1)}, u32[]{:S(2)}, u32[]{:S(2)}) %collective-permute-start.1) | collective-permute-done | bytes 135200 | tf_op jit(solution)/shard_map/ppermute | solution.py:207
  47.2 0.0 all-to-all-done
  47.3 1.4 %select.1 = (f32[256,1024]{1,0:T(8,128)S(1)}, f32[8,128]{1,0:T(8,128)S(1)}) custom-call(f32[640,128]{1,0:T(8,128)S(1)} %bitcast.11, s32[1,8]{1,0:T(1,128)} %list_ref.3, f32[33,1024]{1,0:T(8,128)S(1)} %collective-permute-done.1.left_ref, f32[33,1024]{1,0:T(8,128)S(1)} %pad_maximum_fusion.own_ref, f32[33,1024]{1,0:T(8,128)S(1)} %collective-permute-done.2.right_ref), custom_call_target="tpu_custom_call" | custom-call | tf_op jit(solution)/shard_map/select/pallas_call | solution.py:91
  48.7 29.1 %all_to_all.31 = f32[8,32,1024]{2,1,0:T(8,128)S(1)} all-to-all(f32[8,32,1024]{2,1,0:T(8,128)S(1)} %bitcast.14), channel_id=1, replica_groups=mesh['half'=2,'ring'=8,'reg'=32] {'ring'}, dimensions={0} | all-to-all | bytes 2097152 | tf_op jit(solution)/shard_map/all_to_all | solution.py:210
  77.8 6.7 %analyse.1 = f32[256,256]{1,0:T(8,128)S(1)} custom-call(f32[256,1024]{1,0:T(8,128)S(1)} %bitcast.10, f32[8,128]{1,0:T(8,128)S(1)} %get-tuple-element.8.innov_ref, f32[8,128]{1,0:T(8,128)} %bitcast.17, f32[640,128]{1,0:T(8,128)S(1)} %bitcast.12), custom_call_target="tpu_custom_call" | custom-call | tf_op jit(solution)/shard_map/analyse/pallas_call | solution.py:188
  84.6 16.9 %all_to_all.32 = f32[16,16,256]{2,1,0:T(8,128)S(1)} all-to-all(f32[16,16,256]{2,1,0:T(8,128)S(1)} %bitcast.13), channel_id=1, replica_groups=mesh['half'=2,'ring'=8,'reg'=32] {'half','ring'}, dimensions={0} | all-to-all | bytes 524288 | tf_op jit(solution)/shard_map/all_to_all | solution.py:212
  101.5 0.7 copy.7
  (1 shorter events, 0.0 us)
Async XLA Ops:
  1.7 16.1 %copy-start = (f32[16,1024]{1,0:T(8,128)S(1)}, f32[16,1024]{1,0:T(8,128)}, u32[]{:S(2)}) copy-start(f32[16,1024]{1,0:T(8,128)} %param.6) | copy-start | bytes 196612
  1.7 31.1 %copy-start.1 = (f32[1024]{0:T(1024)S(1)}, f32[1024]{0:T(1024)}, u32[]{:S(2)}) copy-start(f32[1024]{0:T(1024)} %param.7) | copy-start | bytes 12292
  1.7 45.5 %all-to-all-start = ((f32[16,40,128]{2,1,0:T(8,128)}), f32[16,40,128]{2,1,0:T(8,128)S(1)}, u32[]{:S(2)}, u32[]{:S(2)}) async-start(f32[16,40,128]{2,1,0:T(8,128)} %bitcast), calls=%async_computation | async-start | bytes 655360 | tf_op jit(solution)/shard_map/all_to_all | solution.py:205
  17.8 14.9 %collective-permute-start = (f32[16,1024]{1,0:T(8,128)S(1)}, f32[16,1024]{1,0:T(8,128)S(1)}, u32[]{:S(2)}, u32[]{:S(2)}) collective-permute-start(f32[16,1024]{1,0:T(8,128)S(1)} %copy-done), channel_id=1, source_target_pairs={{0,256},{256,0},{1,257},{257,1},{2,258},{258,2},{3,259},{259,3},{4... | collective-permute-start | bytes 196616 | tf_op jit(solution)/shard_map/ppermute | solution.py:203
  32.8 9.4 %collective-permute-start.2 = (f32[33,1024]{1,0:T(8,128)S(1)}, f32[33,1024]{1,0:T(8,128)S(1)}, u32[]{:S(2)}, u32[]{:S(2)}) collective-permute-start(f32[33,1024]{1,0:T(8,128)S(1)} %pad_maximum_fusion.own_ref), channel_id=1, source_target_pairs={{1,0},{2,1},{3,2},{4,3},{5,4},{6,5},{7,6},{8,7},{9,8},{10,9},{11,1... | collective-permute-start | bytes 405512 | tf_op jit(solution)/shard_map/ppermute | solution.py:208
  37.9 9.3 %collective-permute-start.1 = (f32[33,1024]{1,0:T(8,128)S(1)}, f32[33,1024]{1,0:T(8,128)S(1)}, u32[]{:S(2)}, u32[]{:S(2)}) collective-permute-start(f32[33,1024]{1,0:T(8,128)S(1)} %pad_maximum_fusion.own_ref), channel_id=1, source_target_pairs={{0,1},{1,2},{2,3},{3,4},{4,5},{5,6},{6,7},{7,8},{8,9},{9,10},{10,1... | collective-permute-start | bytes 405512 | tf_op jit(solution)/shard_map/ppermute | solution.py:207

commit v4 on v3

--- a/solution.py
+++ b/solution.py
@@ -28,49 +28,48 @@
 def pack(ensemble, block_list):
     rows, columns = ensemble.shape
     slots = block_list.shape[1]
-    groups = lax.axis_size(MEM)
-    width = columns // groups
+    ring = lax.axis_size("ring")
+    width = columns // (HALVES * ring)
     pieces = width // LANES
-    depth = pieces * rows + TILE
-
-    def kernel(ens_ref, list_ref, out_ref, tile_ref):
-        tile_ref[...] = jnp.zeros_like(tile_ref)
-        tile_ref[0:1, 0:slots] = list_ref[...].astype(F32)
-        tile = tile_ref[...]
-        for patch in range(groups):
-            base = patch * depth
-            for piece in range(pieces):
-                start = patch * width + piece * LANES
-                out_ref[base + piece * rows : base + (piece + 1) * rows, :] = ens_ref[:, start : start + LANES]
-            out_ref[base + pieces * rows : base + depth, :] = tile
+    depth = HALVES * pieces * rows + TILE
+
+    def kernel(ens_ref, list_ref, out_ref):
+        half = lax.axis_index("half")
+        for target in range(ring):
+            at = target * depth
+            for other in range(HALVES):
+                patch = (half ^ other) * ring + target
+                for piece in range(pieces):
+                    start = pl.multiple_of(patch * width + piece * LANES, LANES)
+                    out_ref[at : at + rows, :] = ens_ref[:, pl.ds(start, LANES)]
+                    at += rows
+            out_ref[at : at + TILE, :] = jnp.zeros((TILE, LANES), F32)
+            out_ref[at : at + 1, 0:slots] = list_ref[...].astype(F32)
 
     return pl.pallas_call(
         kernel,
-        out_shape=pltpu.VMEM((groups * depth, LANES), F32),
+        out_shape=pltpu.VMEM((ring * depth, LANES), F32),
         in_specs=whole(2),
         out_specs=pl.BlockSpec(memory_space=pltpu.VMEM),
-        scratch_shapes=[pltpu.VMEM((TILE, LANES), F32)],
         name="pack",
     )(ensemble, block_list)
 
 
-def select(packed, block_list, left, own, right):
+def select(listed, block_list, left, own, right):
     members = own.shape[0] - 1
     obs = own.shape[1]
     blocks = obs // LANES
     slots = block_list.shape[1]
     ring = lax.axis_size("ring")
-    groups = HALVES * ring
-    depth = packed.shape[0] // groups
+    depth = listed.shape[0] // ring
 
     def kernel(
-        packed_ref, list_ref, left_ref, own_ref, right_ref, out_ref, innov_ref, table, innov_table, lists, wanted, sem
+        listed_ref, list_ref, left_ref, own_ref, right_ref, out_ref, innov_ref, table, innov_table, lists, wanted, sem
     ):
-        half = lax.axis_index("half")
         offset = (lax.axis_index("reg") - 1) * blocks
         for source in range(ring):
-            at = pl.multiple_of((half * ring + source) * depth + depth - TILE, TILE)
-            lists[source : source + 1, :] = packed_ref[pl.ds(at, TILE), :][0:1, :].astype(I32) - offset
+            at = (source + 1) * depth - TILE
+            lists[source : source + 1, :] = listed_ref[at : at + 1, :].astype(I32) - offset
         lists[ring : ring + 1, 0:slots] = list_ref[...] - offset
         copy = pltpu.make_async_copy(lists, wanted, sem)
         copy.start()
@@ -104,7 +103,7 @@
             pltpu.SemaphoreType.DMA,
         ],
         name="select",
-    )(*near(packed), block_list, *near(left, own, right))
+    )(*near(listed), block_list, *near(left, own, right))
 
 
 def parts(value):
@@ -119,28 +118,25 @@
     return dot(high1, high2) + (dot(high1, low2) + dot(low1, high2))
 
 
-def analyse(obs, innov, weights, packed, rows):
+def analyse(obs, innov, weights, packed, crossed, rows):
     members, _ = obs.shape
     slots = innov.shape[0]
     groups = members // rows
     ring = groups // HALVES
-    depth = packed.shape[0] // groups
-    pieces = (depth - TILE) // rows
+    depth = packed.shape[0] // ring
+    pieces = (depth - TILE) // (HALVES * rows)
     width = pieces * LANES
 
-    def kernel(obs_ref, innov_ref, weights_ref, packed_ref, out_ref, columns):
+    def kernel(obs_ref, innov_ref, weights_ref, packed_ref, crossed_ref, out_ref, columns):
         half = lax.axis_index("half")
-
-        def member_group(chunk):
-            return (half ^ (chunk % HALVES)) * ring + chunk // HALVES
-
-        for chunk in range(groups):
-            base = member_group(chunk) * depth
+        for source in range(ring):
             for piece in range(pieces):
-                at = pl.multiple_of(base + piece * rows, TILE)
-                columns[chunk * rows : (chunk + 1) * rows, piece * LANES : (piece + 1) * LANES] = packed_ref[
-                    pl.ds(at, rows), :
-                ]
+                lanes = slice(piece * LANES, (piece + 1) * LANES)
+                own = source * depth + piece * rows
+                other = (source * pieces + piece) * rows
+                at = HALVES * source * rows
+                columns[at : at + rows, lanes] = packed_ref[own : own + rows, :]
+                columns[at + rows : at + HALVES * rows, lanes] = crossed_ref[other : other + rows, :]
         root_weights = jnp.sqrt(weights_ref[...])
         gram_matrix = jnp.zeros((members, members), F32)
         cross = jnp.zeros((members, members), F32)
@@ -182,17 +178,18 @@
         shift = ens_mean + jnp.sum(mean_weights * anomalies, axis=0, keepdims=True)
         updated = product(parts(root), parts(anomalies)) + shift
         for chunk in range(groups):
-            at = pl.multiple_of(member_group(chunk) * rows, TILE)
+            group = (half ^ (chunk % HALVES)) * ring + chunk // HALVES
+            at = pl.multiple_of(group * rows, TILE)
             out_ref[pl.ds(at, rows), :] = updated[chunk * rows : (chunk + 1) * rows, :]
 
     return pl.pallas_call(
         kernel,
         out_shape=pltpu.VMEM((members, width), F32),
-        in_specs=whole(4),
+        in_specs=whole(5),
         out_specs=pl.BlockSpec(memory_space=pltpu.VMEM),
         scratch_shapes=[pltpu.VMEM((members, width), F32)],
         name="analyse",
-    )(*near(obs, innov), weights, *near(packed))
+    )(*near(obs, innov), weights, *near(packed, crossed))
 
 
 def on_device(ensemble, obs_pert, innovation, block_list, loc_weights):
@@ -202,13 +199,17 @@
 
     partner = lax.ppermute(obs_pert, "half", [(0, 1), (1, 0)])
     packed = pack(ensemble, block_list)
-    packed = lax.all_to_all(packed, MEM, split_axis=0, concat_axis=0, tiled=True)
+    packed = lax.all_to_all(packed, "ring", split_axis=0, concat_axis=0, tiled=True)
     table = jnp.concatenate([obs_pert, partner, innovation.reshape(1, own_obs)], axis=0)
     left = lax.ppermute(table, "reg", [(i, i + 1) for i in range(regions - 1)])
     right = lax.ppermute(table, "reg", [(i + 1, i) for i in range(regions - 1)])
     chosen, innov = select(packed, block_list, left, table, right)
     obs = lax.all_to_all(chosen, "ring", split_axis=0, concat_axis=0, tiled=True)
-    updated = analyse(obs, innov, weights, packed, rows)
+    ring = lax.axis_size("ring")
+    chunks = packed.reshape(ring, -1, LANES)
+    part = (chunks.shape[1] - TILE) // HALVES
+    crossed = lax.ppermute(chunks[:, part : 2 * part, :].reshape(-1, LANES), "half", [(0, 1), (1, 0)])
+    updated = analyse(obs, innov, weights, packed, crossed, rows)
     sent = lax.all_to_all(updated, MEM, split_axis=0, concat_axis=0, tiled=True)
     return sent.reshape(sent.shape[0] // rows, rows, -1).transpose(1, 0, 2).reshape(rows, -1)
 

time: 103 us -> 102 us (level)
  the two profiles are of different devices: /device:TPU:14 before, /device:TPU:10 now
where the time goes in v4:
time: 102 us; the launch traced here: 101 us
  starting transfers between devices  42.4 us (42%)
  waiting for transfers between devices  24.2 us (24%)
  blocking collectives  23 us (23%)
  Pallas kernels  10.8 us (11%)
    all_to_all x1, blocking collectives, on_device(): sent = lax.all_to_all(updated, MEM, split_axis=0, concat_axis=0, tiled=True)  23 us
    all_to_all x1, waiting for transfers between devices, on_device(): lax.all_to_all(chosen, 'ring', split_axis=0, concat_axis=0, tiled=True)  15.2 us
    ppermute x1, starting transfers between devices, on_device(): partner = lax.ppermute(obs_pert, 'half', [(0, 1), (1, 0)])  10.9 us
    ppermute x1, starting transfers between devices, on_device(): lax.ppermute(chunks[:, part:2 * part, :].reshape(-1, LANES), 'half', [(0,...  8.31 us
    all_to_all x1, starting transfers between devices, on_device(): lax.all_to_all(packed, 'ring', split_axis=0, concat_axis=0, tiled=True)  7.68 us
    all_to_all x1, starting transfers between devices, on_device(): lax.all_to_all(chosen, 'ring', split_axis=0, concat_axis=0, tiled=True)  7.22 us
    pallas_call x1, Pallas kernels, analyse(): pl.pallas_call(kernel, out_shape=pltpu.VMEM((members, width), F32), in_sp...  6.73 us
    ppermute x1, starting transfers between devices, on_device(): right = lax.ppermute(table, 'reg', [(i + 1, i) for i in range(regions - 1)])  6.34 us
  transfers between devices with their start and end apart: 6, of which 5 were waited for; matrix products, arithmetic and copies ran while one was open for 0% of the time, Pallas kernels for 0%

profile of v4, /device:TPU:10, one launch (start us, length us, event | category | flops | bytes accessed | tf_op | source)
XLA Modules:
  0.0 101.3 jit_solution(18126455890390638721)
XLA Ops:
  0.0 1.7 %pack.1 = f32[576,128]{1,0:T(8,128)} custom-call(f32[16,4096]{1,0:T(8,128)} %ens_ref.1, s32[1,8]{1,0:T(1,128)} %list_ref.3), custom_call_target="tpu_custom_call" | custom-call | tf_op jit(solution)/shard_map/pack/pallas_call | solution.py:49
  1.7 0.0 copy-start
  1.7 0.0 copy-start.1
  1.7 7.7 %all-to-all-start = ((f32[8,72,128]{2,1,0:T(8,128)}), f32[8,72,128]{2,1,0:T(8,128)S(1)}, u32[]{:S(2)}, u32[]{:S(2)}) async-start(f32[8,72,128]{2,1,0:T(8,128)} %bitcast), calls=%async_computation | async-start | bytes 589824 | tf_op jit(solution)/shard_map/all_to_all | solution.py:202
  9.4 0.0 copy-done
  9.4 10.9 %collective-permute-start = (f32[16,1024]{1,0:T(8,128)S(1)}, f32[16,1024]{1,0:T(8,128)S(1)}, u32[]{:S(2)}, u32[]{:S(2)}) collective-permute-start(f32[16,1024]{1,0:T(8,128)S(1)} %copy-done), channel_id=1, source_target_pairs={{0,256},{256,0},{1,257},{257,1},{2,258},{258,2},{3,259},{259,3},{4... | collective-permute-start | bytes 196616 | tf_op jit(solution)/shard_map/ppermute | solution.py:200
  20.3 2.4 %collective-permute-done = f32[16,1024]{1,0:T(8,128)S(1)} collective-permute-done((f32[16,1024]{1,0:T(8,128)S(1)}, f32[16,1024]{1,0:T(8,128)S(1)}, u32[]{:S(2)}, u32[]{:S(2)}) %collective-permute-start) | collective-permute-done | bytes 65568 | tf_op jit(solution)/shard_map/ppermute | solution.py:200
  22.7 0.0 copy-done.1
  22.8 1.9 %collective-permute-start.1 = (f32[33,1024]{1,0:T(8,128)S(1)}, f32[33,1024]{1,0:T(8,128)S(1)}, u32[]{:S(2)}, u32[]{:S(2)}) collective-permute-start(f32[33,1024]{1,0:T(8,128)S(1)} %pad_maximum_fusion.own_ref), channel_id=1, source_target_pairs={{0,1},{1,2},{2,3},{3,4},{4,5},{5,6},{6,7},{7,8},{8,9},{9,10},{10,1... | collective-permute-start | bytes 405512 | tf_op jit(solution)/shard_map/ppermute | solution.py:204
  24.7 6.3 %collective-permute-start.2 = (f32[33,1024]{1,0:T(8,128)S(1)}, f32[33,1024]{1,0:T(8,128)S(1)}, u32[]{:S(2)}, u32[]{:S(2)}) collective-permute-start(f32[33,1024]{1,0:T(8,128)S(1)} %pad_maximum_fusion.own_ref), channel_id=1, source_target_pairs={{1,0},{2,1},{3,2},{4,3},{5,4},{6,5},{7,6},{8,7},{9,8},{10,9},{11,1... | collective-permute-start | bytes 405512 | tf_op jit(solution)/shard_map/ppermute | solution.py:205
  31.0 1.1 %collective-permute-done.1.left_ref = f32[33,1024]{1,0:T(8,128)S(1)} collective-permute-done((f32[33,1024]{1,0:T(8,128)S(1)}, f32[33,1024]{1,0:T(8,128)S(1)}, u32[]{:S(2)}, u32[]{:S(2)}) %collective-permute-start.1) | collective-permute-done | bytes 135200 | tf_op jit(solution)/shard_map/ppermute | solution.py:204
  32.1 1.7 %collective-permute-done.2.right_ref = f32[33,1024]{1,0:T(8,128)S(1)} collective-permute-done((f32[33,1024]{1,0:T(8,128)S(1)}, f32[33,1024]{1,0:T(8,128)S(1)}, u32[]{:S(2)}, u32[]{:S(2)}) %collective-permute-start.2) | collective-permute-done | bytes 135200 | tf_op jit(solution)/shard_map/ppermute | solution.py:205
  33.9 0.0 all-to-all-done
  33.9 2.4 %select.1 = (f32[256,1024]{1,0:T(8,128)}, f32[8,128]{1,0:T(8,128)S(1)}) custom-call(f32[576,128]{1,0:T(8,128)S(1)} %bitcast.12, s32[1,8]{1,0:T(1,128)} %list_ref.3, f32[33,1024]{1,0:T(8,128)S(1)} %collective-permute-done.1.left_ref, f32[33,1024]{1,0:T(8,128)S(1)} %pad_maximum_fusion.own_ref, f32[33,1024]{1,0:T(8,128)S(1)} %collective-permute-done.2.right_ref), custom_call_target="tpu_custom_call" | custom-call | tf_op jit(solution)/shard_map/select/pallas_call | solution.py:90
  36.3 7.2 %all-to-all-start.1 = ((f32[8,32,1024]{2,1,0:T(8,128)}), f32[8,32,1024]{2,1,0:T(8,128)S(1)}, u32[]{:S(2)}, u32[]{:S(2)}) async-start(f32[8,32,1024]{2,1,0:T(8,128)} %bitcast.3), calls=%async_computation.1 | async-start | bytes 2097152 | tf_op jit(solution)/shard_map/all_to_all | solution.py:207
  43.5 8.3 %collective-permute-start.3 = (f32[256,128]{1,0:T(8,128)S(1)}, f32[256,128]{1,0:T(8,128)S(1)}, u32[]{:S(2)}, u32[]{:S(2)}) collective-permute-start(f32[256,128]{1,0:T(8,128)S(1)} %bitcast.16), channel_id=1, source_target_pairs={{0,256},{256,0},{1,257},{257,1},{2,258},{258,2},{3,259},{259,3},{4... | collective-permute-start | bytes 393224 | tf_op jit(solution)/shard_map/ppermute | solution.py:211
  51.8 3.7 %collective-permute-done.3.crossed_ref = f32[256,128]{1,0:T(8,128)S(1)} collective-permute-done((f32[256,128]{1,0:T(8,128)S(1)}, f32[256,128]{1,0:T(8,128)S(1)}, u32[]{:S(2)}, u32[]{:S(2)}) %collective-permute-start.3) | collective-permute-done | bytes 131104 | tf_op jit(solution)/shard_map/ppermute | solution.py:211
  55.5 15.2 %all-to-all-done.1 = f32[8,32,1024]{2,1,0:T(8,128)S(1)} async-done(((f32[8,32,1024]{2,1,0:T(8,128)}), f32[8,32,1024]{2,1,0:T(8,128)S(1)}, u32[]{:S(2)}, u32[]{:S(2)}) %all-to-all-start.1) | async-done | bytes 1048608 | tf_op jit(solution)/shard_map/all_to_all | solution.py:207
  70.8 6.7 %analyse.1 = f32[256,256]{1,0:T(8,128)S(1)} custom-call(f32[256,1024]{1,0:T(8,128)S(1)} %bitcast.11, f32[8,128]{1,0:T(8,128)S(1)} %get-tuple-element.8.innov_ref, f32[8,128]{1,0:T(8,128)} %bitcast.18, f32[576,128]{1,0:T(8,128)S(1)} %bitcast.13, f32[256,128]{1,0:T(8,128)S(1)} %collective-permute-done.3.crossed_ref), custom_call_target="tpu_custom_call" | custom-call | tf_op jit(solution)/shard_map/analyse/pallas_call | solution.py:185
  77.5 23.0 %all_to_all.31 = f32[16,16,256]{2,1,0:T(8,128)S(1)} all-to-all(f32[16,16,256]{2,1,0:T(8,128)S(1)} %bitcast.14), channel_id=1, replica_groups=mesh['half'=2,'ring'=8,'reg'=32] {'half','ring'}, dimensions={0} | all-to-all | bytes 524288 | tf_op jit(solution)/shard_map/all_to_all | solution.py:213
  100.5 0.7 copy.7
  (2 shorter events, 0.0 us)
Async XLA Ops:
  1.7 7.7 %copy-start = (f32[16,1024]{1,0:T(8,128)S(1)}, f32[16,1024]{1,0:T(8,128)}, u32[]{:S(2)}) copy-start(f32[16,1024]{1,0:T(8,128)} %param.6) | copy-start | bytes 196612
  1.7 21.0 %copy-start.1 = (f32[1024]{0:T(1024)S(1)}, f32[1024]{0:T(1024)}, u32[]{:S(2)}) copy-start(f32[1024]{0:T(1024)} %param.7) | copy-start | bytes 12292
  1.7 32.2 %all-to-all-start = ((f32[8,72,128]{2,1,0:T(8,128)}), f32[8,72,128]{2,1,0:T(8,128)S(1)}, u32[]{:S(2)}, u32[]{:S(2)}) async-start(f32[8,72,128]{2,1,0:T(8,128)} %bitcast), calls=%async_computation | async-start | bytes 589824 | tf_op jit(solution)/shard_map/all_to_all | solution.py:202
  9.4 13.4 %collective-permute-start = (f32[16,1024]{1,0:T(8,128)S(1)}, f32[16,1024]{1,0:T(8,128)S(1)}, u32[]{:S(2)}, u32[]{:S(2)}) collective-permute-start(f32[16,1024]{1,0:T(8,128)S(1)} %copy-done), channel_id=1, source_target_pairs={{0,256},{256,0},{1,257},{257,1},{2,258},{258,2},{3,259},{259,3},{4... | collective-permute-start | bytes 196616 | tf_op jit(solution)/shard_map/ppermute | solution.py:200
  22.8 9.4 %collective-permute-start.1 = (f32[33,1024]{1,0:T(8,128)S(1)}, f32[33,1024]{1,0:T(8,128)S(1)}, u32[]{:S(2)}, u32[]{:S(2)}) collective-permute-start(f32[33,1024]{1,0:T(8,128)S(1)} %pad_maximum_fusion.own_ref), channel_id=1, source_target_pairs={{0,1},{1,2},{2,3},{3,4},{4,5},{5,6},{6,7},{7,8},{8,9},{9,10},{10,1... | collective-permute-start | bytes 405512 | tf_op jit(solution)/shard_map/ppermute | solution.py:204
  24.7 9.2 %collective-permute-start.2 = (f32[33,1024]{1,0:T(8,128)S(1)}, f32[33,1024]{1,0:T(8,128)S(1)}, u32[]{:S(2)}, u32[]{:S(2)}) collective-permute-start(f32[33,1024]{1,0:T(8,128)S(1)} %pad_maximum_fusion.own_ref), channel_id=1, source_target_pairs={{1,0},{2,1},{3,2},{4,3},{5,4},{6,5},{7,6},{8,7},{9,8},{10,9},{11,1... | collective-permute-start | bytes 405512 | tf_op jit(solution)/shard_map/ppermute | solution.py:205
  36.3 34.5 %all-to-all-start.1 = ((f32[8,32,1024]{2,1,0:T(8,128)}), f32[8,32,1024]{2,1,0:T(8,128)S(1)}, u32[]{:S(2)}, u32[]{:S(2)}) async-start(f32[8,32,1024]{2,1,0:T(8,128)} %bitcast.3), calls=%async_computation.1 | async-start | bytes 2097152 | tf_op jit(solution)/shard_map/all_to_all | solution.py:207
  43.5 12.0 %collective-permute-start.3 = (f32[256,128]{1,0:T(8,128)S(1)}, f32[256,128]{1,0:T(8,128)S(1)}, u32[]{:S(2)}, u32[]{:S(2)}) collective-permute-start(f32[256,128]{1,0:T(8,128)S(1)} %bitcast.16), channel_id=1, source_target_pairs={{0,256},{256,0},{1,257},{257,1},{2,258},{258,2},{3,259},{259,3},{4... | collective-permute-start | bytes 393224 | tf_op jit(solution)/shard_map/ppermute | solution.py:211

commit v5 on v4

--- a/solution.py
+++ b/solution.py
@@ -52,10 +52,10 @@
         in_specs=whole(2),
         out_specs=pl.BlockSpec(memory_space=pltpu.VMEM),
         name="pack",
-    )(ensemble, block_list)
-
-
-def select(listed, block_list, left, own, right):
+    )(*near(ensemble), block_list)
+
+
+def select(listed, block_list, own, near_side, far_side):
     members = own.shape[0] - 1
     obs = own.shape[1]
     blocks = obs // LANES
@@ -64,16 +64,18 @@
     depth = listed.shape[0] // ring
 
     def kernel(
-        listed_ref, list_ref, left_ref, own_ref, right_ref, out_ref, innov_ref, table, innov_table, lists, wanted, sem
+        listed_ref, list_ref, own_ref, near_ref, far_ref, out_ref, innov_ref, table, innov_table, lists, wanted, sem
     ):
-        offset = (lax.axis_index("reg") - 1) * blocks
+        region = lax.axis_index("reg")
+        offset = (region - 1) * blocks
+        odd = lax.rem(region, 2)
         for source in range(ring):
             at = (source + 1) * depth - TILE
             lists[source : source + 1, :] = listed_ref[at : at + 1, :].astype(I32) - offset
         lists[ring : ring + 1, 0:slots] = list_ref[...] - offset
         copy = pltpu.make_async_copy(lists, wanted, sem)
         copy.start()
-        for side, ref in enumerate((left_ref, own_ref, right_ref)):
+        for side, ref in ((1, own_ref), (2 - 2 * odd, near_ref), (2 * odd, far_ref)):
             for block in range(blocks):
                 at = side * blocks + block
                 table[at] = ref[0:members, block * LANES : (block + 1) * LANES]
@@ -103,7 +105,7 @@
             pltpu.SemaphoreType.DMA,
         ],
         name="select",
-    )(*near(listed), block_list, *near(left, own, right))
+    )(*near(listed), block_list, *near(own, near_side, far_side))
 
 
 def parts(value):
@@ -201,9 +203,10 @@
     packed = pack(ensemble, block_list)
     packed = lax.all_to_all(packed, "ring", split_axis=0, concat_axis=0, tiled=True)
     table = jnp.concatenate([obs_pert, partner, innovation.reshape(1, own_obs)], axis=0)
-    left = lax.ppermute(table, "reg", [(i, i + 1) for i in range(regions - 1)])
-    right = lax.ppermute(table, "reg", [(i + 1, i) for i in range(regions - 1)])
-    chosen, innov = select(packed, block_list, left, table, right)
+    swaps = [[(i + a, i + 1 - a) for i in range(first, regions - 1, 2) for a in (0, 1)] for first in (0, 1)]
+    far_side = lax.ppermute(table, "reg", swaps[1])
+    near_side = lax.ppermute(table, "reg", swaps[0])
+    chosen, innov = select(packed, block_list, table, near_side, far_side)
     obs = lax.all_to_all(chosen, "ring", split_axis=0, concat_axis=0, tiled=True)
     ring = lax.axis_size("ring")
     chunks = packed.reshape(ring, -1, LANES)

time: 102 us -> 101 us (level)
  the two profiles are of different devices: /device:TPU:10 before, /device:TPU:76 now
where the time goes in v5:
time: 101 us; the launch traced here: 100 us
  starting transfers between devices  36.4 us (36%)
  waiting for transfers between devices  27.9 us (28%)
  blocking collectives  23.5 us (23%)
  Pallas kernels  10.5 us (10%)
  local copies, waits for them, and re-layouts  1.69 us (2%)
    all_to_all x1, blocking collectives, on_device(): sent = lax.all_to_all(updated, MEM, split_axis=0, concat_axis=0, tiled=True)  23.5 us
    all_to_all x1, waiting for transfers between devices, on_device(): lax.all_to_all(chosen, 'ring', split_axis=0, concat_axis=0, tiled=True)  13.3 us
    ppermute x1, starting transfers between devices, on_device(): partner = lax.ppermute(obs_pert, 'half', [(0, 1), (1, 0)])  10 us
    all_to_all x1, starting transfers between devices, on_device(): lax.all_to_all(packed, 'ring', split_axis=0, concat_axis=0, tiled=True)  7.68 us
    ppermute x1, starting transfers between devices, on_device(): lax.ppermute(chunks[:, part:2 * part, :].reshape(-1, LANES), 'half', [(0,...  7.64 us
    all_to_all x1, starting transfers between devices, on_device(): lax.all_to_all(chosen, 'ring', split_axis=0, concat_axis=0, tiled=True)  7.22 us
    ppermute x1, waiting for transfers between devices, on_device(): lax.ppermute(chunks[:, part:2 * part, :].reshape(-1, LANES), 'half', [(0,...  6.78 us
    pallas_call x1, Pallas kernels, analyse(): pl.pallas_call(kernel, out_shape=pltpu.VMEM((members, width), F32), in_sp...  6.72 us
  transfers between devices with their start and end apart: 6, of which 4 were waited for; matrix products, arithmetic and copies ran while one was open for 0% of the time, Pallas kernels for 0%

profile of v5, /device:TPU:76, one launch (start us, length us, event | category | flops | bytes accessed | tf_op | source)
XLA Modules:
  0.0 100.1 jit_solution(11025975142692507234)
XLA Ops:
  0.0 0.0 copy-start
  0.0 0.9 copy-done
  1.0 1.4 %pack.1 = f32[576,128]{1,0:T(8,128)} custom-call(f32[16,4096]{1,0:T(8,128)S(1)} %copy-done, s32[1,8]{1,0:T(1,128)} %list_ref.3), custom_call_target="tpu_custom_call" | custom-call | tf_op jit(solution)/shard_map/pack/pallas_call | solution.py:49
  2.4 0.0 copy-start.1
  2.4 0.0 copy-start.2
  2.4 7.7 %all-to-all-start = ((f32[8,72,128]{2,1,0:T(8,128)}), f32[8,72,128]{2,1,0:T(8,128)S(1)}, u32[]{:S(2)}, u32[]{:S(2)}) async-start(f32[8,72,128]{2,1,0:T(8,128)} %bitcast), calls=%async_computation | async-start | bytes 589824 | tf_op jit(solution)/shard_map/all_to_all | solution.py:204
  10.0 0.0 copy-done.1
  10.0 10.0 %collective-permute-start = (f32[16,1024]{1,0:T(8,128)S(1)}, f32[16,1024]{1,0:T(8,128)S(1)}, u32[]{:S(2)}, u32[]{:S(2)}) collective-permute-start(f32[16,1024]{1,0:T(8,128)S(1)} %copy-done.1), channel_id=1, source_target_pairs={{0,256},{256,0},{1,257},{257,1},{2,258},{258,2},{3,259},{259,3},{4... | collective-permute-start | bytes 196616 | tf_op jit(solution)/shard_map/ppermute | solution.py:202
  20.0 3.0 %collective-permute-done = f32[16,1024]{1,0:T(8,128)S(1)} collective-permute-done((f32[16,1024]{1,0:T(8,128)S(1)}, f32[16,1024]{1,0:T(8,128)S(1)}, u32[]{:S(2)}, u32[]{:S(2)}) %collective-permute-start) | collective-permute-done | bytes 65568 | tf_op jit(solution)/shard_map/ppermute | solution.py:202
  23.1 0.0 copy-done.2
  23.1 1.9 %collective-permute-start.1 = (f32[33,1024]{1,0:T(8,128)S(1)}, f32[33,1024]{1,0:T(8,128)S(1)}, u32[]{:S(2)}, u32[]{:S(2)}) collective-permute-start(f32[33,1024]{1,0:T(8,128)S(1)} %pad_maximum_fusion.own_ref), channel_id=1, source_target_pairs={{0,1},{1,0},{2,3},{3,2},{4,5},{5,4},{6,7},{7,6},{8,9},{9,8},{10,11... | collective-permute-start | bytes 405512 | tf_op jit(solution)/shard_map/ppermute | solution.py:208
  25.0 2.0 %collective-permute-start.2 = (f32[33,1024]{1,0:T(8,128)S(1)}, f32[33,1024]{1,0:T(8,128)S(1)}, u32[]{:S(2)}, u32[]{:S(2)}) collective-permute-start(f32[33,1024]{1,0:T(8,128)S(1)} %pad_maximum_fusion.own_ref), channel_id=1, source_target_pairs={{1,2},{2,1},{3,4},{4,3},{5,6},{6,5},{7,8},{8,7},{9,10},{10,9},{11,... | collective-permute-start | bytes 405512 | tf_op jit(solution)/shard_map/ppermute | solution.py:207
  27.0 0.0 collective-permute-done.1.near_ref
  27.0 4.7 %collective-permute-done.2.far_ref = f32[33,1024]{1,0:T(8,128)S(1)} collective-permute-done((f32[33,1024]{1,0:T(8,128)S(1)}, f32[33,1024]{1,0:T(8,128)S(1)}, u32[]{:S(2)}, u32[]{:S(2)}) %collective-permute-start.2) | collective-permute-done | bytes 135200 | tf_op jit(solution)/shard_map/ppermute | solution.py:207
  31.8 0.0 all-to-all-done
  31.8 2.4 %select.1 = (f32[256,1024]{1,0:T(8,128)}, f32[8,128]{1,0:T(8,128)S(1)}) custom-call(f32[576,128]{1,0:T(8,128)S(1)} %bitcast.12, s32[1,8]{1,0:T(1,128)} %list_ref.3, f32[33,1024]{1,0:T(8,128)S(1)} %pad_maximum_fusion.own_ref, f32[33,1024]{1,0:T(8,128)S(1)} %collective-permute-done.1.near_ref, f32[33,1024]{1,0:T(8,128)S(1)} %collective-permute-done.2.far_ref), custom_call_target="tpu_custom_call" | custom-call | tf_op jit(solution)/shard_map/select/pallas_call | solution.py:92
  34.2 7.2 %all-to-all-start.1 = ((f32[8,32,1024]{2,1,0:T(8,128)}), f32[8,32,1024]{2,1,0:T(8,128)S(1)}, u32[]{:S(2)}, u32[]{:S(2)}) async-start(f32[8,32,1024]{2,1,0:T(8,128)} %bitcast.3), calls=%async_computation.1 | async-start | bytes 2097152 | tf_op jit(solution)/shard_map/all_to_all | solution.py:210
  41.4 7.6 %collective-permute-start.3 = (f32[256,128]{1,0:T(8,128)S(1)}, f32[256,128]{1,0:T(8,128)S(1)}, u32[]{:S(2)}, u32[]{:S(2)}) collective-permute-start(f32[256,128]{1,0:T(8,128)S(1)} %bitcast.16), channel_id=1, source_target_pairs={{0,256},{256,0},{1,257},{257,1},{2,258},{258,2},{3,259},{259,3},{4... | collective-permute-start | bytes 393224 | tf_op jit(solution)/shard_map/ppermute | solution.py:214
  49.0 6.8 %collective-permute-done.3.crossed_ref = f32[256,128]{1,0:T(8,128)S(1)} collective-permute-done((f32[256,128]{1,0:T(8,128)S(1)}, f32[256,128]{1,0:T(8,128)S(1)}, u32[]{:S(2)}, u32[]{:S(2)}) %collective-permute-start.3) | collective-permute-done | bytes 131104 | tf_op jit(solution)/shard_map/ppermute | solution.py:214
  55.8 13.3 %all-to-all-done.1 = f32[8,32,1024]{2,1,0:T(8,128)S(1)} async-done(((f32[8,32,1024]{2,1,0:T(8,128)}), f32[8,32,1024]{2,1,0:T(8,128)S(1)}, u32[]{:S(2)}, u32[]{:S(2)}) %all-to-all-start.1) | async-done | bytes 1048608 | tf_op jit(solution)/shard_map/all_to_all | solution.py:210
  69.1 6.7 %analyse.1 = f32[256,256]{1,0:T(8,128)S(1)} custom-call(f32[256,1024]{1,0:T(8,128)S(1)} %bitcast.11, f32[8,128]{1,0:T(8,128)S(1)} %get-tuple-element.8.innov_ref, f32[8,128]{1,0:T(8,128)} %bitcast.18, f32[576,128]{1,0:T(8,128)S(1)} %bitcast.13, f32[256,128]{1,0:T(8,128)S(1)} %collective-permute-done.3.crossed_ref), custom_call_target="tpu_custom_call" | custom-call | tf_op jit(solution)/shard_map/analyse/pallas_call | solution.py:187
  75.9 23.5 %all_to_all.31 = f32[16,16,256]{2,1,0:T(8,128)S(1)} all-to-all(f32[16,16,256]{2,1,0:T(8,128)S(1)} %bitcast.14), channel_id=1, replica_groups=mesh['half'=2,'ring'=8,'reg'=32] {'half','ring'}, dimensions={0} | all-to-all | bytes 524288 | tf_op jit(solution)/shard_map/all_to_all | solution.py:216
  99.4 0.7 copy.7
  (2 shorter events, 0.0 us)
Async XLA Ops:
  0.0 0.9 copy-start
  2.4 7.7 %copy-start.1 = (f32[16,1024]{1,0:T(8,128)S(1)}, f32[16,1024]{1,0:T(8,128)}, u32[]{:S(2)}) copy-start(f32[16,1024]{1,0:T(8,128)} %param.6) | copy-start | bytes 196612
  2.4 20.7 %copy-start.2 = (f32[1024]{0:T(1024)S(1)}, f32[1024]{0:T(1024)}, u32[]{:S(2)}) copy-start(f32[1024]{0:T(1024)} %param.7) | copy-start | bytes 12292
  2.4 29.4 %all-to-all-start = ((f32[8,72,128]{2,1,0:T(8,128)}), f32[8,72,128]{2,1,0:T(8,128)S(1)}, u32[]{:S(2)}, u32[]{:S(2)}) async-start(f32[8,72,128]{2,1,0:T(8,128)} %bitcast), calls=%async_computation | async-start | bytes 589824 | tf_op jit(solution)/shard_map/all_to_all | solution.py:204
  10.0 13.0 %collective-permute-start = (f32[16,1024]{1,0:T(8,128)S(1)}, f32[16,1024]{1,0:T(8,128)S(1)}, u32[]{:S(2)}, u32[]{:S(2)}) collective-permute-start(f32[16,1024]{1,0:T(8,128)S(1)} %copy-done.1), channel_id=1, source_target_pairs={{0,256},{256,0},{1,257},{257,1},{2,258},{258,2},{3,259},{259,3},{4... | collective-permute-start | bytes 196616 | tf_op jit(solution)/shard_map/ppermute | solution.py:202
  23.1 3.9 %collective-permute-start.1 = (f32[33,1024]{1,0:T(8,128)S(1)}, f32[33,1024]{1,0:T(8,128)S(1)}, u32[]{:S(2)}, u32[]{:S(2)}) collective-permute-start(f32[33,1024]{1,0:T(8,128)S(1)} %pad_maximum_fusion.own_ref), channel_id=1, source_target_pairs={{0,1},{1,0},{2,3},{3,2},{4,5},{5,4},{6,7},{7,6},{8,9},{9,8},{10,11... | collective-permute-start | bytes 405512 | tf_op jit(solution)/shard_map/ppermute | solution.py:208
  25.0 6.7 %collective-permute-start.2 = (f32[33,1024]{1,0:T(8,128)S(1)}, f32[33,1024]{1,0:T(8,128)S(1)}, u32[]{:S(2)}, u32[]{:S(2)}) collective-permute-start(f32[33,1024]{1,0:T(8,128)S(1)} %pad_maximum_fusion.own_ref), channel_id=1, source_target_pairs={{1,2},{2,1},{3,4},{4,3},{5,6},{6,5},{7,8},{8,7},{9,10},{10,9},{11,... | collective-permute-start | bytes 405512 | tf_op jit(solution)/shard_map/ppermute | solution.py:207
  34.2 35.0 %all-to-all-start.1 = ((f32[8,32,1024]{2,1,0:T(8,128)}), f32[8,32,1024]{2,1,0:T(8,128)S(1)}, u32[]{:S(2)}, u32[]{:S(2)}) async-start(f32[8,32,1024]{2,1,0:T(8,128)} %bitcast.3), calls=%async_computation.1 | async-start | bytes 2097152 | tf_op jit(solution)/shard_map/all_to_all | solution.py:210
  41.4 14.4 %collective-permute-start.3 = (f32[256,128]{1,0:T(8,128)S(1)}, f32[256,128]{1,0:T(8,128)S(1)}, u32[]{:S(2)}, u32[]{:S(2)}) collective-permute-start(f32[256,128]{1,0:T(8,128)S(1)} %bitcast.16), channel_id=1, source_target_pairs={{0,256},{256,0},{1,257},{257,1},{2,258},{258,2},{3,259},{259,3},{4... | collective-permute-start | bytes 393224 | tf_op jit(solution)/shard_map/ppermute | solution.py:214

commit v6 on v5

v6 whole, which is shorter than its diff:
```python
import jax
import jax.numpy as jnp
from jax import lax
from jax.experimental import pallas as pl
from jax.experimental.pallas import tpu as pltpu
from jax.sharding import Mesh
from jax.sharding import PartitionSpec as P


NEWTON = 8
LANES = 128
TILE = 8
HALVES = 2
FIXED = 2
F32 = jnp.float32
BF16 = jnp.bfloat16
I32 = jnp.int32
MEM = ("half", "ring")


def whole(count):
    return [pl.BlockSpec(memory_space=pltpu.VMEM)] * count


def near(*arrays):
    return [pltpu.with_memory_space_constraint(value, pltpu.VMEM) for value in arrays]


def pack(ensemble, obs_pert, block_list):
    rows, columns = ensemble.shape
    obs = obs_pert.shape[1]
    slots = block_list.shape[1]
    ring = lax.axis_size("ring")
    width = columns // (HALVES * ring)
    pieces = width // LANES
    depth = (HALVES * pieces + FIXED) * rows + TILE

    def kernel(ens_ref, obs_ref, list_ref, out_ref):
        half = lax.axis_index("half")
        for target in range(ring):
            at = target * depth
            for other in range(HALVES):
                patch = (half ^ other) * ring + target
                for piece in range(pieces):
                    start = pl.multiple_of(patch * width + piece * LANES, LANES)
                    out_ref[at : at + rows, :] = ens_ref[:, pl.ds(start, LANES)]
                    at += rows
            for start in (0, obs - LANES):
                out_ref[at : at + rows, :] = obs_ref[:, start : start + LANES]
                at += rows
            out_ref[at : at + TILE, :] = jnp.zeros((TILE, LANES), F32)
            out_ref[at : at + 1, 0:slots] = list_ref[...].astype(F32)

    return pl.pallas_call(
        kernel,
        out_shape=pltpu.VMEM((ring * depth, LANES), F32),
        in_specs=whole(3),
        out_specs=pl.BlockSpec(memory_space=pltpu.VMEM),
        name="pack",
    )(ensemble, obs_pert, block_list)


def select(listed, block_list, weights, own, near_side, far_side):
    members = own.shape[0] - 1
    blocks = own.shape[1] // LANES
    slots = block_list.shape[1]
    others = slots - FIXED
    ring = lax.axis_size("ring")
    depth = listed.shape[0] // ring
    fixed = (blocks, 2 * blocks - 1)

    def kernel(
        listed_ref, list_ref, weights_ref, own_ref, near_ref, far_ref, out_ref, scales_ref,
        table, innov_table, lists, staged, wanted, rest, list_sem, sems,
    ):
        region = lax.axis_index("reg")
        offset = (region - 1) * blocks
        odd = lax.rem(region, 2)
        for source in range(ring):
            at = (source + 1) * depth - TILE
            lists[source : source + 1, :] = listed_ref[at : at + 1, :].astype(I32) - offset
        lists[ring : ring + 1, 0:slots] = list_ref[...] - offset
        copy = pltpu.make_async_copy(lists, wanted, list_sem)
        copy.start()
        for side, ref in ((1, own_ref), (2 - 2 * odd, near_ref), (2 * odd, far_ref)):
            for block in range(blocks):
                at = side * blocks + block
                table[at] = ref[0:members, block * LANES : (block + 1) * LANES]
                innov_table[at] = ref[members : members + 1, block * LANES : (block + 1) * LANES]
        copy.wait()

        def compact(patch, order):
            count = jnp.int32(0)
            places = [jnp.int32(0)] * FIXED
            for slot in range(slots):
                block = wanted[patch, slot]
                rest[order, count] = block
                if order:
                    rest[2, count] = jnp.int32(slot)
                    places = [jnp.where(block == f, slot, at) for f, at in zip(fixed, places)]
                found = [block == f for f in fixed]
                count = count + jnp.where(found[0] | found[1], 0, 1)
            return places

        copies = []
        for patch in range(ring):
            compact(patch, 0)
            for slot in range(others):
                staged[patch * members : (patch + 1) * members, slot * LANES : (slot + 1) * LANES] = table[rest[0, slot]]
            span = pl.ds(patch * members, members)
            copies.append(pltpu.make_async_copy(staged.at[span], out_ref.at[span], sems.at[patch]))
            copies[-1].start()
        places = compact(ring, 1)
        for slot in range(others):
            scales_ref[slot : slot + 1, :] = innov_table[rest[1, slot]]
            scales_ref[slots + slot : slots + slot + 1, :] = weights_ref[pl.ds(rest[2, slot], 1), :]
        for which in range(FIXED):
            slot = others + which
            scales_ref[slot : slot + 1, :] = innov_table[fixed[which]]
            scales_ref[slots + slot : slots + slot + 1, :] = weights_ref[pl.ds(places[which], 1), :]
        for copy in copies:
            copy.wait()

    return pl.pallas_call(
        kernel,
        out_shape=(
            jax.ShapeDtypeStruct((ring * members, others * LANES), F32),
            pltpu.VMEM((2 * slots, LANES), F32),
        ),
        in_specs=whole(6),
        out_specs=(pl.BlockSpec(memory_space=pl.ANY), pl.BlockSpec(memory_space=pltpu.VMEM)),
        scratch_shapes=[
            pltpu.VMEM((3 * blocks, members, LANES), F32),
            pltpu.VMEM((3 * blocks, 1, LANES), F32),
            pltpu.VMEM((2 * TILE, LANES), I32),
            pltpu.VMEM((ring * members, others * LANES), F32),
            pltpu.SMEM((2 * TILE, LANES), I32),
            pltpu.SMEM((3, slots), I32),
            pltpu.SemaphoreType.DMA,
            pltpu.SemaphoreType.DMA((ring,)),
        ],
        name="select",
    )(*near(listed), block_list, *near(weights, own, near_side, far_side))


def parts(value):
    high = value.astype(BF16)
    return high, (value - high.astype(F32)).astype(BF16)


def product(first, second):
    high1, low1 = first
    high2, low2 = second
    dot = lambda a, b: jnp.dot(a, b, preferred_element_type=F32)
    return dot(high1, high2) + (dot(high1, low2) + dot(low1, high2))


def analyse(obs, scales, packed, crossed, rows):
    members, _ = obs.shape
    slots = scales.shape[0] // 2
    others = slots - FIXED
    groups = members // rows
    ring = groups // HALVES
    depth = packed.shape[0] // ring
    strips = crossed.shape[0] // (ring * rows)
    pieces = strips - FIXED
    width = pieces * LANES

    def kernel(obs_ref, scales_ref, packed_ref, crossed_ref, out_ref, columns):
        half = lax.axis_index("half")
        for source in range(ring):
            for strip in range(strips):
                lanes = slice(strip * LANES, (strip + 1) * LANES)
                skip = strip if strip < pieces else strip + pieces
                own = source * depth + skip * rows
                other = (source * strips + strip) * rows
                at = HALVES * source * rows
                columns[at : at + rows, lanes] = packed_ref[own : own + rows, :]
                columns[at + rows : at + HALVES * rows, lanes] = crossed_ref[other : other + rows, :]
        root_weights = jnp.sqrt(scales_ref[slots : 2 * slots, :])
        gram_matrix = jnp.zeros((members, members), F32)
        cross = jnp.zeros((members, members), F32)
        drive = jnp.zeros((members, LANES), F32)
        contract = lambda a, b: lax.dot_general(
            a, b, (((1,), (1,)), ((), ())), preferred_element_type=F32
        )
        for slot in range(slots):
            if slot < others:
                block = obs_ref[:, slot * LANES : (slot + 1) * LANES]
            else:
                block = columns[:, width + (slot - others) * LANES : width + (slot - others + 1) * LANES]
            scaled = block * root_weights[slot : slot + 1, :]
            drive += scaled * (root_weights[slot : slot + 1, :] * scales_ref[slot : slot + 1, :])
            high, low = parts(scaled)
            gram_matrix += contract(high, high)
            cross += contract(high, low)
        gram_matrix += cross + cross.T
        drive = jnp.sum(drive, axis=1, keepdims=True)
        identity = (
            lax.broadcasted_iota(I32, (members, members), 0) == lax.broadcasted_iota(I32, (members, members), 1)
        ).astype(F32)
        system = identity + gram_matrix / (members - 1.0)
        trace_sum = jnp.sum(system * identity, keepdims=True)
        iterate_y = system / trace_sum
        half_three = 1.5 * identity
        factor = half_three - 0.5 * iterate_y
        y_parts = parts(iterate_y)
        z_parts = parts(factor)
        y_parts = parts(product(y_parts, z_parts))
        for repeat in range(1, NEWTON):
            factor = parts(half_three - 0.5 * product(z_parts, y_parts))
            iterate_z = product(factor, z_parts)
            if repeat < NEWTON - 1:
                y_parts = parts(product(y_parts, factor))
                z_parts = parts(iterate_z)
        root = iterate_z / jnp.sqrt(trace_sum)
        half_step = jnp.sum(root * drive, axis=0, keepdims=True)
        mean_weights = jnp.sum(root * half_step, axis=1, keepdims=True) / (members - 1.0)
        ens = columns[:, 0:width]
        ens_mean = jnp.mean(ens, axis=0, keepdims=True)
        anomalies = ens - ens_mean
        shift = ens_mean + jnp.sum(mean_weights * anomalies, axis=0, keepdims=True)
        updated = product(parts(root), parts(anomalies)) + shift
        for chunk in range(groups):
            group = (half ^ (chunk % HALVES)) * ring + chunk // HALVES
            at = pl.multiple_of(group * rows, TILE)
            out_ref[pl.ds(at, rows), :] = updated[chunk * rows : (chunk + 1) * rows, :]

    return pl.pallas_call(
        kernel,
        out_shape=pltpu.VMEM((members, width), F32),
        in_specs=whole(4),
        out_specs=pl.BlockSpec(memory_space=pltpu.VMEM),
        scratch_shapes=[pltpu.VMEM((members, strips * LANES), F32)],
        name="analyse",
    )(*near(obs, scales, packed, crossed))


def on_device(ensemble, obs_pert, innovation, block_list, loc_weights):
    regions = lax.axis_size("reg")
    rows, own_obs = obs_pert.shape
    weights = loc_weights.reshape(loc_weights.shape[1:])

    partner = lax.ppermute(obs_pert, "half", [(0, 1), (1, 0)])
    packed = pack(ensemble, obs_pert, block_list)
    packed = lax.all_to_all(packed, "ring", split_axis=0, concat_axis=0, tiled=True)
    table = jnp.concatenate([obs_pert, partner, innovation.reshape(1, own_obs)], axis=0)
    swaps = [[(i + a, i + 1 - a) for i in range(first, regions - 1, 2) for a in (0, 1)] for first in (0, 1)]
    far_side = lax.ppermute(table, "reg", swaps[1])
    near_side = lax.ppermute(table, "reg", swaps[0])
    chosen, scales = select(packed, block_list, weights, table, near_side, far_side)
    obs = lax.all_to_all(chosen, "ring", split_axis=0, concat_axis=0, tiled=True)
    ring = lax.axis_size("ring")
    chunks = packed.reshape(ring, -1, LANES)
    part = ensemble.shape[1] // (HALVES * ring) // LANES * rows
    crossed = lax.ppermute(chunks[:, part : chunks.shape[1] - TILE, :].reshape(-1, LANES), "half", [(0, 1), (1, 0)])
    updated = analyse(obs, scales, packed, crossed, rows)
    sent = lax.all_to_all(updated, MEM, split_axis=0, concat_axis=0, tiled=True)
    return sent.reshape(sent.shape[0] // rows, rows, -1).transpose(1, 0, 2).reshape(rows, -1)


def solution(mesh):
    groups, regions = (mesh.shape[name] for name in ("mem", "reg"))
    fine = Mesh(mesh.devices.reshape(HALVES, groups // HALVES, regions), MEM + ("reg",))
    return jax.shard_map(
        on_device,
        mesh=fine,
        in_specs=(
            P(MEM, "reg"),
            P(MEM, "reg"),
            P("reg"),
            P(("reg",) + MEM, None),
            P(("reg",) + MEM, None, None),
        ),
        out_specs=P(MEM, "reg"),
        check_vma=False,
    )
```

time: 101 us -> 94.7 us (0.938)
  waiting for transfers between devices: 27.9 us -> 22.2 us
  blocking collectives: 23.5 us -> 24.6 us
    all_to_all x1, waiting for transfers between devices: 13.3 us -> 2.01 us  [on_device(): lax.all_to_all(chosen, 'ring', split_axis=0, concat_axis=0, tiled=True)]
    ppermute x1, waiting for transfers between devices: 6.78 us -> 12.4 us  [on_device(): lax.ppermute(chunks[:, part:chunks.shape[1] - TILE, :].reshape(-1, LANES)...]
    all_to_all x1, blocking collectives: 23.5 us -> 24.6 us  [on_device(): sent = lax.all_to_all(updated, MEM, split_axis=0, concat_axis=0, tiled=True)]
where the time goes in v6:
time: 94.7 us; the launch traced here: 94.3 us
  starting transfers between devices  36.4 us (38%)
  blocking collectives  24.6 us (26%)
  waiting for transfers between devices  22.2 us (23%)
  Pallas kernels  10.2 us (11%)
    all_to_all x1, blocking collectives, on_device(): sent = lax.all_to_all(updated, MEM, split_axis=0, concat_axis=0, tiled=True)  24.6 us
    ppermute x1, waiting for transfers between devices, on_device(): lax.ppermute(chunks[:, part:chunks.shape[1] - TILE, :].reshape(-1, LANES)...  12.4 us
    ppermute x1, starting transfers between devices, on_device(): partner = lax.ppermute(obs_pert, 'half', [(0, 1), (1, 0)])  10 us
    all_to_all x1, starting transfers between devices, on_device(): lax.all_to_all(packed, 'ring', split_axis=0, concat_axis=0, tiled=True)  7.68 us
    ppermute x1, starting transfers between devices, on_device(): lax.ppermute(chunks[:, part:chunks.shape[1] - TILE, :].reshape(-1, LANES)...  7.64 us
    all_to_all x1, starting transfers between devices, on_device(): lax.all_to_all(chosen, 'ring', split_axis=0, concat_axis=0, tiled=True)  7.22 us
    pallas_call x1, Pallas kernels, analyse(): pl.pallas_call(kernel, out_shape=pltpu.VMEM((members, width), F32), in_sp...  6.04 us
    ppermute x1, waiting for transfers between devices, on_device(): far_side = lax.ppermute(table, 'reg', swaps[1])  4.73 us
  transfers between devices with their start and end apart: 6, of which 4 were waited for; matrix products, arithmetic and copies ran while one was open for 0% of the time, Pallas kernels for 0%

profile of v6, /device:TPU:76, one launch (start us, length us, event | category | flops | bytes accessed | tf_op | source)
XLA Modules:
  0.0 94.3 jit_solution(14432323514681864751)
XLA Ops:
  0.0 1.8 %pack.1 = f32[832,128]{1,0:T(8,128)} custom-call(f32[16,4096]{1,0:T(8,128)} %ens_ref.1, f32[16,1024]{1,0:T(8,128)} %obs_ref.1, s32[1,8]{1,0:T(1,128)} %list_ref.3), custom_call_target="tpu_custom_call" | custom-call | tf_op jit(solution)/shard_map/pack/pallas_call | solution.py:54
  1.8 0.0 copy-start.1
  1.8 0.0 copy-start.2
  1.8 7.7 %all-to-all-start = ((f32[8,104,128]{2,1,0:T(8,128)}), f32[8,104,128]{2,1,0:T(8,128)S(1)}, u32[]{:S(2)}, u32[]{:S(2)}) async-start(f32[8,104,128]{2,1,0:T(8,128)} %bitcast), calls=%async_computation | async-start | bytes 851968 | tf_op jit(solution)/shard_map/all_to_all | solution.py:246
  9.5 0.0 copy-done.1
  9.5 10.0 %collective-permute-start = (f32[16,1024]{1,0:T(8,128)S(1)}, f32[16,1024]{1,0:T(8,128)S(1)}, u32[]{:S(2)}, u32[]{:S(2)}) collective-permute-start(f32[16,1024]{1,0:T(8,128)S(1)} %copy-done.1), channel_id=1, source_target_pairs={{0,256},{256,0},{1,257},{257,1},{2,258},{258,2},{3,259},{259,3},{4... | collective-permute-start | bytes 196616 | tf_op jit(solution)/shard_map/ppermute | solution.py:244
  19.5 3.0 %collective-permute-done = f32[16,1024]{1,0:T(8,128)S(1)} collective-permute-done((f32[16,1024]{1,0:T(8,128)S(1)}, f32[16,1024]{1,0:T(8,128)S(1)}, u32[]{:S(2)}, u32[]{:S(2)}) %collective-permute-start) | collective-permute-done | bytes 65568 | tf_op jit(solution)/shard_map/ppermute | solution.py:244
  22.5 0.0 copy-done.2
  22.5 0.0 copy-start
  22.5 1.9 %collective-permute-start.1 = (f32[33,1024]{1,0:T(8,128)S(1)}, f32[33,1024]{1,0:T(8,128)S(1)}, u32[]{:S(2)}, u32[]{:S(2)}) collective-permute-start(f32[33,1024]{1,0:T(8,128)S(1)} %pad_maximum_fusion.own_ref), channel_id=1, source_target_pairs={{0,1},{1,0},{2,3},{3,2},{4,5},{5,4},{6,7},{7,6},{8,9},{9,8},{10,11... | collective-permute-start | bytes 405512 | tf_op jit(solution)/shard_map/ppermute | solution.py:250
  24.5 2.0 %collective-permute-start.2 = (f32[33,1024]{1,0:T(8,128)S(1)}, f32[33,1024]{1,0:T(8,128)S(1)}, u32[]{:S(2)}, u32[]{:S(2)}) collective-permute-start(f32[33,1024]{1,0:T(8,128)S(1)} %pad_maximum_fusion.own_ref), channel_id=1, source_target_pairs={{1,2},{2,1},{3,4},{4,3},{5,6},{6,5},{7,8},{8,7},{9,10},{10,9},{11,... | collective-permute-start | bytes 405512 | tf_op jit(solution)/shard_map/ppermute | solution.py:249
  26.5 0.0 collective-permute-done.1.near_ref
  26.5 4.7 %collective-permute-done.2.far_ref = f32[33,1024]{1,0:T(8,128)S(1)} collective-permute-done((f32[33,1024]{1,0:T(8,128)S(1)}, f32[33,1024]{1,0:T(8,128)S(1)}, u32[]{:S(2)}, u32[]{:S(2)}) %collective-permute-start.2) | collective-permute-done | bytes 135200 | tf_op jit(solution)/shard_map/ppermute | solution.py:249
  31.2 0.0 all-to-all-done
  31.2 0.0 copy-done
  31.2 2.3 %select.1 = (f32[256,768]{1,0:T(8,128)}, f32[16,128]{1,0:T(8,128)S(1)}) custom-call(f32[832,128]{1,0:T(8,128)S(1)} %bitcast.11, s32[1,8]{1,0:T(1,128)} %list_ref.3, f32[8,128]{1,0:T(8,128)S(1)} %bitcast.15, f32[33,1024]{1,0:T(8,128)S(1)} %pad_maximum_fusion.own_ref, f32[33,1024]{1,0:T(8,128)S(1)} %collective-permute-done.1.near_ref, ...), custom_call_target="tpu_custom_call" | custom-call | tf_op jit(solution)/shard_map/select/pallas_call | solution.py:124
  33.6 7.2 %all-to-all-start.1 = ((f32[8,32,768]{2,1,0:T(8,128)}), f32[8,32,768]{2,1,0:T(8,128)S(1)}, u32[]{:S(2)}, u32[]{:S(2)}) async-start(f32[8,32,768]{2,1,0:T(8,128)} %bitcast.17), calls=%async_computation.1 | async-start | bytes 1572864 | tf_op jit(solution)/shard_map/all_to_all | solution.py:252
  40.8 7.6 %collective-permute-start.3 = (f32[512,128]{1,0:T(8,128)S(1)}, f32[512,128]{1,0:T(8,128)S(1)}, u32[]{:S(2)}, u32[]{:S(2)}) collective-permute-start(f32[512,128]{1,0:T(8,128)S(1)} %bitcast.18), channel_id=1, source_target_pairs={{0,256},{256,0},{1,257},{257,1},{2,258},{258,2},{3,259},{259,3},{4... | collective-permute-start | bytes 786440 | tf_op jit(solution)/shard_map/ppermute | solution.py:256
  48.4 12.4 %collective-permute-done.3.crossed_ref = f32[512,128]{1,0:T(8,128)S(1)} collective-permute-done((f32[512,128]{1,0:T(8,128)S(1)}, f32[512,128]{1,0:T(8,128)S(1)}, u32[]{:S(2)}, u32[]{:S(2)}) %collective-permute-start.3) | collective-permute-done | bytes 262176 | tf_op jit(solution)/shard_map/ppermute | solution.py:256
  60.9 2.0 %all-to-all-done.1 = f32[8,32,768]{2,1,0:T(8,128)S(1)} async-done(((f32[8,32,768]{2,1,0:T(8,128)}), f32[8,32,768]{2,1,0:T(8,128)S(1)}, u32[]{:S(2)}, u32[]{:S(2)}) %all-to-all-start.1) | async-done | bytes 786464 | tf_op jit(solution)/shard_map/all_to_all | solution.py:252
  62.9 6.0 %analyse.1 = f32[256,256]{1,0:T(8,128)S(1)} custom-call(f32[256,768]{1,0:T(8,128)S(1)} %bitcast.13, f32[16,128]{1,0:T(8,128)S(1)} %get-tuple-element.8.scales_ref, f32[832,128]{1,0:T(8,128)S(1)} %bitcast.12, f32[512,128]{1,0:T(8,128)S(1)} %collective-permute-done.3.crossed_ref), custom_call_target="tpu_custom_call" | custom-call | tf_op jit(solution)/shard_map/analyse/pallas_call | solution.py:229
  68.9 24.6 %all_to_all.31 = f32[16,16,256]{2,1,0:T(8,128)S(1)} all-to-all(f32[16,16,256]{2,1,0:T(8,128)S(1)} %bitcast.14), channel_id=1, replica_groups=mesh['half'=2,'ring'=8,'reg'=32] {'half','ring'}, dimensions={0} | all-to-all | bytes 524288 | tf_op jit(solution)/shard_map/all_to_all | solution.py:258
  93.6 0.7 copy.7
  (2 shorter events, 0.0 us)
Async XLA Ops:
  1.8 7.7 %copy-start.1 = (f32[16,1024]{1,0:T(8,128)S(1)}, f32[16,1024]{1,0:T(8,128)}, u32[]{:S(2)}) copy-start(f32[16,1024]{1,0:T(8,128)} %obs_ref.1) | copy-start | bytes 196612
  1.8 20.7 %copy-start.2 = (f32[1024]{0:T(1024)S(1)}, f32[1024]{0:T(1024)}, u32[]{:S(2)}) copy-start(f32[1024]{0:T(1024)} %param.7) | copy-start | bytes 12292
  1.8 29.4 %all-to-all-start = ((f32[8,104,128]{2,1,0:T(8,128)}), f32[8,104,128]{2,1,0:T(8,128)S(1)}, u32[]{:S(2)}, u32[]{:S(2)}) async-start(f32[8,104,128]{2,1,0:T(8,128)} %bitcast), calls=%async_computation | async-start | bytes 851968 | tf_op jit(solution)/shard_map/all_to_all | solution.py:246
  9.5 13.0 %collective-permute-start = (f32[16,1024]{1,0:T(8,128)S(1)}, f32[16,1024]{1,0:T(8,128)S(1)}, u32[]{:S(2)}, u32[]{:S(2)}) collective-permute-start(f32[16,1024]{1,0:T(8,128)S(1)} %copy-done.1), channel_id=1, source_target_pairs={{0,256},{256,0},{1,257},{257,1},{2,258},{258,2},{3,259},{259,3},{4... | collective-permute-start | bytes 196616 | tf_op jit(solution)/shard_map/ppermute | solution.py:244
  22.5 8.7 %copy-start = (f32[1,8,128]{2,1,0:T(8,128)S(1)}, f32[1,8,128]{2,1,0:T(8,128)}, u32[]{:S(2)}) copy-start(f32[1,8,128]{2,1,0:T(8,128)} %param.9) | copy-start | bytes 12292
  22.5 3.9 %collective-permute-start.1 = (f32[33,1024]{1,0:T(8,128)S(1)}, f32[33,1024]{1,0:T(8,128)S(1)}, u32[]{:S(2)}, u32[]{:S(2)}) collective-permute-start(f32[33,1024]{1,0:T(8,128)S(1)} %pad_maximum_fusion.own_ref), channel_id=1, source_target_pairs={{0,1},{1,0},{2,3},{3,2},{4,5},{5,4},{6,7},{7,6},{8,9},{9,8},{10,11... | collective-permute-start | bytes 405512 | tf_op jit(solution)/shard_map/ppermute | solution.py:250
  24.5 6.7 %collective-permute-start.2 = (f32[33,1024]{1,0:T(8,128)S(1)}, f32[33,1024]{1,0:T(8,128)S(1)}, u32[]{:S(2)}, u32[]{:S(2)}) collective-permute-start(f32[33,1024]{1,0:T(8,128)S(1)} %pad_maximum_fusion.own_ref), channel_id=1, source_target_pairs={{1,2},{2,1},{3,4},{4,3},{5,6},{6,5},{7,8},{8,7},{9,10},{10,9},{11,... | collective-permute-start | bytes 405512 | tf_op jit(solution)/shard_map/ppermute | solution.py:249
  33.6 29.3 %all-to-all-start.1 = ((f32[8,32,768]{2,1,0:T(8,128)}), f32[8,32,768]{2,1,0:T(8,128)S(1)}, u32[]{:S(2)}, u32[]{:S(2)}) async-start(f32[8,32,768]{2,1,0:T(8,128)} %bitcast.17), calls=%async_computation.1 | async-start | bytes 1572864 | tf_op jit(solution)/shard_map/all_to_all | solution.py:252
  40.8 20.1 %collective-permute-start.3 = (f32[512,128]{1,0:T(8,128)S(1)}, f32[512,128]{1,0:T(8,128)S(1)}, u32[]{:S(2)}, u32[]{:S(2)}) collective-permute-start(f32[512,128]{1,0:T(8,128)S(1)} %bitcast.18), channel_id=1, source_target_pairs={{0,256},{256,0},{1,257},{257,1},{2,258},{258,2},{3,259},{259,3},{4... | collective-permute-start | bytes 786440 | tf_op jit(solution)/shard_map/ppermute | solution.py:256

commit v7 on v6

--- a/solution.py
+++ b/solution.py
@@ -35,42 +35,63 @@
     pieces = width // LANES
     depth = (HALVES * pieces + FIXED) * rows + TILE
 
-    def kernel(ens_ref, obs_ref, list_ref, out_ref):
+    strips = HALVES * pieces + FIXED
+
+    def kernel(ens_ref, obs_ref, list_ref, out_ref, listed, tile, list_sem, sems):
         half = lax.axis_index("half")
+        fetch = pltpu.make_async_copy(list_ref, listed, list_sem)
+        fetch.start()
+        copies = []
+
+        def send(source, at, size):
+            copy = pltpu.make_async_copy(source, out_ref.at[at : at + size], sems.at[len(copies)])
+            copy.start()
+            copies.append(copy)
+
         for target in range(ring):
             at = target * depth
             for other in range(HALVES):
                 patch = (half ^ other) * ring + target
                 for piece in range(pieces):
                     start = pl.multiple_of(patch * width + piece * LANES, LANES)
-                    out_ref[at : at + rows, :] = ens_ref[:, pl.ds(start, LANES)]
+                    send(ens_ref.at[:, pl.ds(start, LANES)], at, rows)
                     at += rows
             for start in (0, obs - LANES):
-                out_ref[at : at + rows, :] = obs_ref[:, start : start + LANES]
+                send(obs_ref.at[:, start : start + LANES], at, rows)
                 at += rows
-            out_ref[at : at + TILE, :] = jnp.zeros((TILE, LANES), F32)
-            out_ref[at : at + 1, 0:slots] = list_ref[...].astype(F32)
+        tile[...] = jnp.zeros_like(tile)
+        fetch.wait()
+        tile[0:1, 0:slots] = listed[...].astype(F32)
+        for target in range(ring):
+            send(tile, (target + 1) * depth - TILE, TILE)
+        for copy in copies:
+            copy.wait()
 
     return pl.pallas_call(
         kernel,
-        out_shape=pltpu.VMEM((ring * depth, LANES), F32),
-        in_specs=whole(3),
-        out_specs=pl.BlockSpec(memory_space=pltpu.VMEM),
+        out_shape=jax.ShapeDtypeStruct((ring * depth, LANES), F32),
+        in_specs=[pl.BlockSpec(memory_space=pl.ANY)] * 3,
+        out_specs=pl.BlockSpec(memory_space=pl.ANY),
+        scratch_shapes=[
+            pltpu.VMEM((1, slots), I32),
+            pltpu.VMEM((TILE, LANES), F32),
+            pltpu.SemaphoreType.DMA,
+            pltpu.SemaphoreType.DMA((ring * (strips + 1),)),
+        ],
         name="pack",
     )(ensemble, obs_pert, block_list)
 
 
-def select(listed, block_list, weights, own, near_side, far_side):
+def select(listed, slots, weights, own, near_side, far_side):
     members = own.shape[0] - 1
     blocks = own.shape[1] // LANES
-    slots = block_list.shape[1]
     others = slots - FIXED
     ring = lax.axis_size("ring")
     depth = listed.shape[0] // ring
     fixed = (blocks, 2 * blocks - 1)
 
     def kernel(
-        listed_ref, list_ref, weights_ref, own_ref, near_ref, far_ref, out_ref, scales_ref,
+        listed_ref, weights_ref, own_ref, near_ref, far_ref, out_ref, scales_ref,
         table, innov_table, lists, staged, wanted, rest, list_sem, sems,
     ):
         region = lax.axis_index("reg")
@@ -79,7 +100,6 @@
         for source in range(ring):
             at = (source + 1) * depth - TILE
             lists[source : source + 1, :] = listed_ref[at : at + 1, :].astype(I32) - offset
-        lists[ring : ring + 1, 0:slots] = list_ref[...] - offset
         copy = pltpu.make_async_copy(lists, wanted, list_sem)
         copy.start()
         for side, ref in ((1, own_ref), (2 - 2 * odd, near_ref), (2 * odd, far_ref)):
@@ -110,7 +130,7 @@
             span = pl.ds(patch * members, members)
             copies.append(pltpu.make_async_copy(staged.at[span], out_ref.at[span], sems.at[patch]))
             copies[-1].start()
-        places = compact(ring, 1)
+        places = compact(lax.axis_index("ring"), 1)
         for slot in range(others):
             scales_ref[slot : slot + 1, :] = innov_table[rest[1, slot]]
             scales_ref[slots + slot : slots + slot + 1, :] = weights_ref[pl.ds(rest[2, slot], 1), :]
@@ -127,20 +147,20 @@
             jax.ShapeDtypeStruct((ring * members, others * LANES), F32),
             pltpu.VMEM((2 * slots, LANES), F32),
         ),
-        in_specs=whole(6),
+        in_specs=whole(5),
         out_specs=(pl.BlockSpec(memory_space=pl.ANY), pl.BlockSpec(memory_space=pltpu.VMEM)),
         scratch_shapes=[
             pltpu.VMEM((3 * blocks, members, LANES), F32),
             pltpu.VMEM((3 * blocks, 1, LANES), F32),
-            pltpu.VMEM((2 * TILE, LANES), I32),
+            pltpu.VMEM((ring, LANES), I32),
             pltpu.VMEM((ring * members, others * LANES), F32),
-            pltpu.SMEM((2 * TILE, LANES), I32),
+            pltpu.SMEM((ring, LANES), I32),
             pltpu.SMEM((3, slots), I32),
             pltpu.SemaphoreType.DMA,
             pltpu.SemaphoreType.DMA((ring,)),
         ],
         name="select",
-    )(*near(listed), block_list, *near(weights, own, near_side, far_side))
+    )(*near(listed, weights, own, near_side, far_side))
 
 
 def parts(value):
@@ -178,12 +198,11 @@
                 columns[at : at + rows, lanes] = packed_ref[own : own + rows, :]
                 columns[at + rows : at + HALVES * rows, lanes] = crossed_ref[other : other + rows, :]
         root_weights = jnp.sqrt(scales_ref[slots : 2 * slots, :])
-        gram_matrix = jnp.zeros((members, members), F32)
-        cross = jnp.zeros((members, members), F32)
         drive = jnp.zeros((members, LANES), F32)
         contract = lambda a, b: lax.dot_general(
             a, b, (((1,), (1,)), ((), ())), preferred_element_type=F32
         )
+        highs, lows = [], []
         for slot in range(slots):
             if slot < others:
                 block = obs_ref[:, slot * LANES : (slot + 1) * LANES]
@@ -192,8 +211,11 @@
             scaled = block * root_weights[slot : slot + 1, :]
             drive += scaled * (root_weights[slot : slot + 1, :] * scales_ref[slot : slot + 1, :])
             high, low = parts(scaled)
-            gram_matrix += contract(high, high)
-            cross += contract(high, low)
+            highs.append(high)
+            lows.append(low)
+        high = jnp.concatenate(highs, axis=1)
+        gram_matrix = contract(high, high)
+        cross = contract(high, jnp.concatenate(lows, axis=1))
         gram_matrix += cross + cross.T
         drive = jnp.sum(drive, axis=1, keepdims=True)
         identity = (
@@ -248,7 +270,7 @@
     swaps = [[(i + a, i + 1 - a) for i in range(first, regions - 1, 2) for a in (0, 1)] for first in (0, 1)]
     far_side = lax.ppermute(table, "reg", swaps[1])
     near_side = lax.ppermute(table, "reg", swaps[0])
-    chosen, scales = select(packed, block_list, weights, table, near_side, far_side)
+    chosen, scales = select(packed, block_list.shape[1], weights, table, near_side, far_side)
     obs = lax.all_to_all(chosen, "ring", split_axis=0, concat_axis=0, tiled=True)
     ring = lax.axis_size("ring")
     chunks = packed.reshape(ring, -1, LANES)

time: 94.7 us -> 106 us (1.12)
  Pallas kernels: 10.2 us -> 21 us
    pallas_call x1, Pallas kernels: 1.79 us -> 13.5 us  [pack(): pl.pallas_call(kernel, out_shape=jax.ShapeDtypeStruct((ring * depth, LANE...]
where the time goes in v7:
time: 106 us; the launch traced here: 105 us
  starting transfers between devices  36.5 us (34%)
  blocking collectives  24.6 us (23%)
  waiting for transfers between devices  22.2 us (21%)
  Pallas kernels  21 us (20%)
    all_to_all x1, blocking collectives, on_device(): sent = lax.all_to_all(updated, MEM, split_axis=0, concat_axis=0, tiled=True)  24.6 us
    pallas_call x1, Pallas kernels, pack(): pl.pallas_call(kernel, out_shape=jax.ShapeDtypeStruct((ring * depth, LANE...  13.5 us
    ppermute x1, waiting for transfers between devices, on_device(): lax.ppermute(chunks[:, part:chunks.shape[1] - TILE, :].reshape(-1, LANES)...  12.4 us
    ppermute x1, starting transfers between devices, on_device(): partner = lax.ppermute(obs_pert, 'half', [(0, 1), (1, 0)])  10 us
    all_to_all x1, starting transfers between devices, on_device(): lax.all_to_all(packed, 'ring', split_axis=0, concat_axis=0, tiled=True)  7.69 us
    ppermute x1, starting transfers between devices, on_device(): lax.ppermute(chunks[:, part:chunks.shape[1] - TILE, :].reshape(-1, LANES)...  7.64 us
    all_to_all x1, starting transfers between devices, on_device(): lax.all_to_all(chosen, 'ring', split_axis=0, concat_axis=0, tiled=True)  7.22 us
    pallas_call x1, Pallas kernels, analyse(): pl.pallas_call(kernel, out_shape=pltpu.VMEM((members, width), F32), in_sp...  5.81 us
  transfers between devices with their start and end apart: 6, of which 4 were waited for; matrix products, arithmetic and copies ran while one was open for 0% of the time, Pallas kernels for 0%

profile of v7, /device:TPU:76, one launch (start us, length us, event | category | flops | bytes accessed | tf_op | source)
XLA Modules:
  0.0 105.1 jit_solution(9202509890441680655)
XLA Ops:
  0.0 13.5 %pack.1 = f32[832,128]{1,0:T(8,128)} custom-call(f32[16,4096]{1,0:T(8,128)} %ens_ref.1, f32[16,1024]{1,0:T(8,128)} %obs_ref.1, s32[1,8]{1,0:T(1,128)} %list_ref.1), custom_call_target="tpu_custom_call" | custom-call | tf_op jit(solution)/shard_map/pack/pallas_call | solution.py:70
  13.6 0.0 copy-start.1
  13.6 0.0 copy-start.2
  13.6 7.7 %all-to-all-start = ((f32[8,104,128]{2,1,0:T(8,128)}), f32[8,104,128]{2,1,0:T(8,128)S(1)}, u32[]{:S(2)}, u32[]{:S(2)}) async-start(f32[8,104,128]{2,1,0:T(8,128)} %bitcast.16), calls=%async_computation | async-start | bytes 851968 | tf_op jit(solution)/shard_map/all_to_all | solution.py:268
  21.3 0.0 copy-done.1
  21.3 10.0 %collective-permute-start = (f32[16,1024]{1,0:T(8,128)S(1)}, f32[16,1024]{1,0:T(8,128)S(1)}, u32[]{:S(2)}, u32[]{:S(2)}) collective-permute-start(f32[16,1024]{1,0:T(8,128)S(1)} %copy-done.1), channel_id=1, source_target_pairs={{0,256},{256,0},{1,257},{257,1},{2,258},{258,2},{3,259},{259,3},{4... | collective-permute-start | bytes 196616 | tf_op jit(solution)/shard_map/ppermute | solution.py:266
  31.3 3.0 %collective-permute-done = f32[16,1024]{1,0:T(8,128)S(1)} collective-permute-done((f32[16,1024]{1,0:T(8,128)S(1)}, f32[16,1024]{1,0:T(8,128)S(1)}, u32[]{:S(2)}, u32[]{:S(2)}) %collective-permute-start) | collective-permute-done | bytes 65568 | tf_op jit(solution)/shard_map/ppermute | solution.py:266
  34.3 0.0 copy-done.2
  34.3 0.0 copy-start
  34.3 1.9 %collective-permute-start.1 = (f32[33,1024]{1,0:T(8,128)S(1)}, f32[33,1024]{1,0:T(8,128)S(1)}, u32[]{:S(2)}, u32[]{:S(2)}) collective-permute-start(f32[33,1024]{1,0:T(8,128)S(1)} %pad_maximum_fusion.own_ref), channel_id=1, source_target_pairs={{0,1},{1,0},{2,3},{3,2},{4,5},{5,4},{6,7},{7,6},{8,9},{9,8},{10,11... | collective-permute-start | bytes 405512 | tf_op jit(solution)/shard_map/ppermute | solution.py:272
  36.3 2.0 %collective-permute-start.2 = (f32[33,1024]{1,0:T(8,128)S(1)}, f32[33,1024]{1,0:T(8,128)S(1)}, u32[]{:S(2)}, u32[]{:S(2)}) collective-permute-start(f32[33,1024]{1,0:T(8,128)S(1)} %pad_maximum_fusion.own_ref), channel_id=1, source_target_pairs={{1,2},{2,1},{3,4},{4,3},{5,6},{6,5},{7,8},{8,7},{9,10},{10,9},{11,... | collective-permute-start | bytes 405512 | tf_op jit(solution)/shard_map/ppermute | solution.py:271
  38.3 0.0 collective-permute-done.1.near_ref
  38.3 4.7 %collective-permute-done.2.far_ref = f32[33,1024]{1,0:T(8,128)S(1)} collective-permute-done((f32[33,1024]{1,0:T(8,128)S(1)}, f32[33,1024]{1,0:T(8,128)S(1)}, u32[]{:S(2)}, u32[]{:S(2)}) %collective-permute-start.2) | collective-permute-done | bytes 135200 | tf_op jit(solution)/shard_map/ppermute | solution.py:271
  43.0 0.0 all-to-all-done
  43.0 0.0 copy-done
  43.0 1.6 %select.1 = (f32[256,768]{1,0:T(8,128)}, f32[16,128]{1,0:T(8,128)S(1)}) custom-call(f32[832,128]{1,0:T(8,128)S(1)} %bitcast.11, f32[8,128]{1,0:T(8,128)S(1)} %bitcast.15, f32[33,1024]{1,0:T(8,128)S(1)} %pad_maximum_fusion.own_ref, f32[33,1024]{1,0:T(8,128)S(1)} %collective-permute-done.1.near_ref, f32[33,1024]{1,0:T(8,128)S(1)} %collective-permute-done.2.far_ref), custom_call_target="tpu_custom_call" | custom-call | tf_op jit(solution)/shard_map/select/pallas_call | solution.py:144
  44.6 7.2 %all-to-all-start.1 = ((f32[8,32,768]{2,1,0:T(8,128)}), f32[8,32,768]{2,1,0:T(8,128)S(1)}, u32[]{:S(2)}, u32[]{:S(2)}) async-start(f32[8,32,768]{2,1,0:T(8,128)} %bitcast.18), calls=%async_computation.1 | async-start | bytes 1572864 | tf_op jit(solution)/shard_map/all_to_all | solution.py:274
  51.9 7.6 %collective-permute-start.3 = (f32[512,128]{1,0:T(8,128)S(1)}, f32[512,128]{1,0:T(8,128)S(1)}, u32[]{:S(2)}, u32[]{:S(2)}) collective-permute-start(f32[512,128]{1,0:T(8,128)S(1)} %bitcast.19), channel_id=1, source_target_pairs={{0,256},{256,0},{1,257},{257,1},{2,258},{258,2},{3,259},{259,3},{4... | collective-permute-start | bytes 786440 | tf_op jit(solution)/shard_map/ppermute | solution.py:278
  59.5 12.4 %collective-permute-done.3.crossed_ref = f32[512,128]{1,0:T(8,128)S(1)} collective-permute-done((f32[512,128]{1,0:T(8,128)S(1)}, f32[512,128]{1,0:T(8,128)S(1)}, u32[]{:S(2)}, u32[]{:S(2)}) %collective-permute-start.3) | collective-permute-done | bytes 262176 | tf_op jit(solution)/shard_map/ppermute | solution.py:278
  72.0 2.0 %all-to-all-done.1 = f32[8,32,768]{2,1,0:T(8,128)S(1)} async-done(((f32[8,32,768]{2,1,0:T(8,128)}), f32[8,32,768]{2,1,0:T(8,128)S(1)}, u32[]{:S(2)}, u32[]{:S(2)}) %all-to-all-start.1) | async-done | bytes 786464 | tf_op jit(solution)/shard_map/all_to_all | solution.py:274
  74.0 5.8 %analyse.1 = f32[256,256]{1,0:T(8,128)S(1)} custom-call(f32[256,768]{1,0:T(8,128)S(1)} %bitcast.13, f32[16,128]{1,0:T(8,128)S(1)} %get-tuple-element.8.scales_ref, f32[832,128]{1,0:T(8,128)S(1)} %bitcast.12, f32[512,128]{1,0:T(8,128)S(1)} %collective-permute-done.3.crossed_ref), custom_call_target="tpu_custom_call" | custom-call | tf_op jit(solution)/shard_map/analyse/pallas_call | solution.py:251
  79.8 24.6 %all_to_all.31 = f32[16,16,256]{2,1,0:T(8,128)S(1)} all-to-all(f32[16,16,256]{2,1,0:T(8,128)S(1)} %bitcast.14), channel_id=1, replica_groups=mesh['half'=2,'ring'=8,'reg'=32] {'half','ring'}, dimensions={0} | all-to-all | bytes 524288 | tf_op jit(solution)/shard_map/all_to_all | solution.py:280
  104.4 0.7 copy.7
  (2 shorter events, 0.0 us)
Async XLA Ops:
  13.6 7.7 %copy-start.1 = (f32[16,1024]{1,0:T(8,128)S(1)}, f32[16,1024]{1,0:T(8,128)}, u32[]{:S(2)}) copy-start(f32[16,1024]{1,0:T(8,128)} %obs_ref.1) | copy-start | bytes 196612
  13.6 20.8 %copy-start.2 = (f32[1024]{0:T(1024)S(1)}, f32[1024]{0:T(1024)}, u32[]{:S(2)}) copy-start(f32[1024]{0:T(1024)} %param.7) | copy-start | bytes 12292
  13.6 29.4 %all-to-all-start = ((f32[8,104,128]{2,1,0:T(8,128)}), f32[8,104,128]{2,1,0:T(8,128)S(1)}, u32[]{:S(2)}, u32[]{:S(2)}) async-start(f32[8,104,128]{2,1,0:T(8,128)} %bitcast.16), calls=%async_computation | async-start | bytes 851968 | tf_op jit(solution)/shard_map/all_to_all | solution.py:268
  21.3 13.0 %collective-permute-start = (f32[16,1024]{1,0:T(8,128)S(1)}, f32[16,1024]{1,0:T(8,128)S(1)}, u32[]{:S(2)}, u32[]{:S(2)}) collective-permute-start(f32[16,1024]{1,0:T(8,128)S(1)} %copy-done.1), channel_id=1, source_target_pairs={{0,256},{256,0},{1,257},{257,1},{2,258},{258,2},{3,259},{259,3},{4... | collective-permute-start | bytes 196616 | tf_op jit(solution)/shard_map/ppermute | solution.py:266
  34.3 8.7 %copy-start = (f32[1,8,128]{2,1,0:T(8,128)S(1)}, f32[1,8,128]{2,1,0:T(8,128)}, u32[]{:S(2)}) copy-start(f32[1,8,128]{2,1,0:T(8,128)} %param.9) | copy-start | bytes 12292
  34.3 3.9 %collective-permute-start.1 = (f32[33,1024]{1,0:T(8,128)S(1)}, f32[33,1024]{1,0:T(8,128)S(1)}, u32[]{:S(2)}, u32[]{:S(2)}) collective-permute-start(f32[33,1024]{1,0:T(8,128)S(1)} %pad_maximum_fusion.own_ref), channel_id=1, source_target_pairs={{0,1},{1,0},{2,3},{3,2},{4,5},{5,4},{6,7},{7,6},{8,9},{9,8},{10,11... | collective-permute-start | bytes 405512 | tf_op jit(solution)/shard_map/ppermute | solution.py:272
  36.3 6.7 %collective-permute-start.2 = (f32[33,1024]{1,0:T(8,128)S(1)}, f32[33,1024]{1,0:T(8,128)S(1)}, u32[]{:S(2)}, u32[]{:S(2)}) collective-permute-start(f32[33,1024]{1,0:T(8,128)S(1)} %pad_maximum_fusion.own_ref), channel_id=1, source_target_pairs={{1,2},{2,1},{3,4},{4,3},{5,6},{6,5},{7,8},{8,7},{9,10},{10,9},{11,... | collective-permute-start | bytes 405512 | tf_op jit(solution)/shard_map/ppermute | solution.py:271
  44.6 29.3 %all-to-all-start.1 = ((f32[8,32,768]{2,1,0:T(8,128)}), f32[8,32,768]{2,1,0:T(8,128)S(1)}, u32[]{:S(2)}, u32[]{:S(2)}) async-start(f32[8,32,768]{2,1,0:T(8,128)} %bitcast.18), calls=%async_computation.1 | async-start | bytes 1572864 | tf_op jit(solution)/shard_map/all_to_all | solution.py:274
  51.9 20.1 %collective-permute-start.3 = (f32[512,128]{1,0:T(8,128)S(1)}, f32[512,128]{1,0:T(8,128)S(1)}, u32[]{:S(2)}, u32[]{:S(2)}) collective-permute-start(f32[512,128]{1,0:T(8,128)S(1)} %bitcast.19), channel_id=1, source_target_pairs={{0,256},{256,0},{1,257},{257,1},{2,258},{258,2},{3,259},{259,3},{4... | collective-permute-start | bytes 786440 | tf_op jit(solution)/shard_map/ppermute | solution.py:278

commit v8 on v6

--- a/solution.py
+++ b/solution.py
@@ -60,17 +60,16 @@
     )(ensemble, obs_pert, block_list)
 
 
-def select(listed, block_list, weights, own, near_side, far_side):
+def select(listed, slots, weights, own, near_side, far_side):
     members = own.shape[0] - 1
     blocks = own.shape[1] // LANES
-    slots = block_list.shape[1]
     others = slots - FIXED
     ring = lax.axis_size("ring")
     depth = listed.shape[0] // ring
     fixed = (blocks, 2 * blocks - 1)
 
     def kernel(
-        listed_ref, list_ref, weights_ref, own_ref, near_ref, far_ref, out_ref, scales_ref,
+        listed_ref, weights_ref, own_ref, near_ref, far_ref, out_ref, scales_ref,
         table, innov_table, lists, staged, wanted, rest, list_sem, sems,
     ):
         region = lax.axis_index("reg")
@@ -79,7 +78,6 @@
         for source in range(ring):
             at = (source + 1) * depth - TILE
             lists[source : source + 1, :] = listed_ref[at : at + 1, :].astype(I32) - offset
-        lists[ring : ring + 1, 0:slots] = list_ref[...] - offset
         copy = pltpu.make_async_copy(lists, wanted, list_sem)
         copy.start()
         for side, ref in ((1, own_ref), (2 - 2 * odd, near_ref), (2 * odd, far_ref)):
@@ -110,7 +108,7 @@
             span = pl.ds(patch * members, members)
             copies.append(pltpu.make_async_copy(staged.at[span], out_ref.at[span], sems.at[patch]))
             copies[-1].start()
-        places = compact(ring, 1)
+        places = compact(lax.axis_index("ring"), 1)
         for slot in range(others):
             scales_ref[slot : slot + 1, :] = innov_table[rest[1, slot]]
             scales_ref[slots + slot : slots + slot + 1, :] = weights_ref[pl.ds(rest[2, slot], 1), :]
@@ -127,20 +125,20 @@
             jax.ShapeDtypeStruct((ring * members, others * LANES), F32),
             pltpu.VMEM((2 * slots, LANES), F32),
         ),
-        in_specs=whole(6),
+        in_specs=whole(5),
         out_specs=(pl.BlockSpec(memory_space=pl.ANY), pl.BlockSpec(memory_space=pltpu.VMEM)),
         scratch_shapes=[
             pltpu.VMEM((3 * blocks, members, LANES), F32),
             pltpu.VMEM((3 * blocks, 1, LANES), F32),
-            pltpu.VMEM((2 * TILE, LANES), I32),
+            pltpu.VMEM((ring, LANES), I32),
             pltpu.VMEM((ring * members, others * LANES), F32),
-            pltpu.SMEM((2 * TILE, LANES), I32),
+            pltpu.SMEM((ring, LANES), I32),
             pltpu.SMEM((3, slots), I32),
             pltpu.SemaphoreType.DMA,
             pltpu.SemaphoreType.DMA((ring,)),
         ],
         name="select",
-    )(*near(listed), block_list, *near(weights, own, near_side, far_side))
+    )(*near(listed, weights, own, near_side, far_side))
 
 
 def parts(value):
@@ -178,12 +176,11 @@
                 columns[at : at + rows, lanes] = packed_ref[own : own + rows, :]
                 columns[at + rows : at + HALVES * rows, lanes] = crossed_ref[other : other + rows, :]
         root_weights = jnp.sqrt(scales_ref[slots : 2 * slots, :])
-        gram_matrix = jnp.zeros((members, members), F32)
-        cross = jnp.zeros((members, members), F32)
         drive = jnp.zeros((members, LANES), F32)
         contract = lambda a, b: lax.dot_general(
             a, b, (((1,), (1,)), ((), ())), preferred_element_type=F32
         )
+        highs, lows = [], []
         for slot in range(slots):
             if slot < others:
                 block = obs_ref[:, slot * LANES : (slot + 1) * LANES]
@@ -192,8 +189,11 @@
             scaled = block * root_weights[slot : slot + 1, :]
             drive += scaled * (root_weights[slot : slot + 1, :] * scales_ref[slot : slot + 1, :])
             high, low = parts(scaled)
-            gram_matrix += contract(high, high)
-            cross += contract(high, low)
+            highs.append(high)
+            lows.append(low)
+        high = jnp.concatenate(highs, axis=1)
+        gram_matrix = contract(high, high)
+        cross = contract(high, jnp.concatenate(lows, axis=1))
         gram_matrix += cross + cross.T
         drive = jnp.sum(drive, axis=1, keepdims=True)
         identity = (
@@ -248,7 +248,7 @@
     swaps = [[(i + a, i + 1 - a) for i in range(first, regions - 1, 2) for a in (0, 1)] for first in (0, 1)]
     far_side = lax.ppermute(table, "reg", swaps[1])
     near_side = lax.ppermute(table, "reg", swaps[0])
-    chosen, scales = select(packed, block_list, weights, table, near_side, far_side)
+    chosen, scales = select(packed, block_list.shape[1], weights, table, near_side, far_side)
     obs = lax.all_to_all(chosen, "ring", split_axis=0, concat_axis=0, tiled=True)
     ring = lax.axis_size("ring")
     chunks = packed.reshape(ring, -1, LANES)

time: 94.7 us -> 93.8 us (level)
  Pallas kernels: 10.2 us -> 9.23 us
where the time goes in v8:
time: 93.8 us; the launch traced here: 93.3 us
  starting transfers between devices  36.4 us (39%)
  blocking collectives  24.6 us (26%)
  waiting for transfers between devices  22.2 us (24%)
  Pallas kernels  9.23 us (10%)
    all_to_all x1, blocking collectives, on_device(): sent = lax.all_to_all(updated, MEM, split_axis=0, concat_axis=0, tiled=True)  24.6 us
    ppermute x1, waiting for transfers between devices, on_device(): lax.ppermute(chunks[:, part:chunks.shape[1] - TILE, :].reshape(-1, LANES)...  12.4 us
    ppermute x1, starting transfers between devices, on_device(): partner = lax.ppermute(obs_pert, 'half', [(0, 1), (1, 0)])  10 us
    all_to_all x1, starting transfers between devices, on_device(): lax.all_to_all(packed, 'ring', split_axis=0, concat_axis=0, tiled=True)  7.68 us
    ppermute x1, starting transfers between devices, on_device(): lax.ppermute(chunks[:, part:chunks.shape[1] - TILE, :].reshape(-1, LANES)...  7.64 us
    all_to_all x1, starting transfers between devices, on_device(): lax.all_to_all(chosen, 'ring', split_axis=0, concat_axis=0, tiled=True)  7.22 us
    pallas_call x1, Pallas kernels, analyse(): pl.pallas_call(kernel, out_shape=pltpu.VMEM((members, width), F32), in_sp...  5.81 us
    ppermute x1, waiting for transfers between devices, on_device(): far_side = lax.ppermute(table, 'reg', swaps[1])  4.73 us
  transfers between devices with their start and end apart: 6, of which 4 were waited for; matrix products, arithmetic and copies ran while one was open for 0% of the time, Pallas kernels for 0%

profile of v8, /device:TPU:76, one launch (start us, length us, event | category | flops | bytes accessed | tf_op | source)
XLA Modules:
  0.0 93.3 jit_solution(17873945580531160821)
XLA Ops:
  0.0 1.8 %pack.1 = f32[832,128]{1,0:T(8,128)} custom-call(f32[16,4096]{1,0:T(8,128)} %ens_ref.1, f32[16,1024]{1,0:T(8,128)} %obs_ref.1, s32[1,8]{1,0:T(1,128)} %list_ref.1), custom_call_target="tpu_custom_call" | custom-call | tf_op jit(solution)/shard_map/pack/pallas_call | solution.py:54
  1.8 0.0 copy-start.1
  1.8 0.0 copy-start.2
  1.8 7.7 %all-to-all-start = ((f32[8,104,128]{2,1,0:T(8,128)}), f32[8,104,128]{2,1,0:T(8,128)S(1)}, u32[]{:S(2)}, u32[]{:S(2)}) async-start(f32[8,104,128]{2,1,0:T(8,128)} %bitcast), calls=%async_computation | async-start | bytes 851968 | tf_op jit(solution)/shard_map/all_to_all | solution.py:246
  9.5 0.0 copy-done.1
  9.5 10.0 %collective-permute-start = (f32[16,1024]{1,0:T(8,128)S(1)}, f32[16,1024]{1,0:T(8,128)S(1)}, u32[]{:S(2)}, u32[]{:S(2)}) collective-permute-start(f32[16,1024]{1,0:T(8,128)S(1)} %copy-done.1), channel_id=1, source_target_pairs={{0,256},{256,0},{1,257},{257,1},{2,258},{258,2},{3,259},{259,3},{4... | collective-permute-start | bytes 196616 | tf_op jit(solution)/shard_map/ppermute | solution.py:244
  19.5 3.0 %collective-permute-done = f32[16,1024]{1,0:T(8,128)S(1)} collective-permute-done((f32[16,1024]{1,0:T(8,128)S(1)}, f32[16,1024]{1,0:T(8,128)S(1)}, u32[]{:S(2)}, u32[]{:S(2)}) %collective-permute-start) | collective-permute-done | bytes 65568 | tf_op jit(solution)/shard_map/ppermute | solution.py:244
  22.5 0.0 copy-done.2
  22.5 0.0 copy-start
  22.5 1.9 %collective-permute-start.1 = (f32[33,1024]{1,0:T(8,128)S(1)}, f32[33,1024]{1,0:T(8,128)S(1)}, u32[]{:S(2)}, u32[]{:S(2)}) collective-permute-start(f32[33,1024]{1,0:T(8,128)S(1)} %pad_maximum_fusion.own_ref), channel_id=1, source_target_pairs={{0,1},{1,0},{2,3},{3,2},{4,5},{5,4},{6,7},{7,6},{8,9},{9,8},{10,11... | collective-permute-start | bytes 405512 | tf_op jit(solution)/shard_map/ppermute | solution.py:250
  24.5 2.0 %collective-permute-start.2 = (f32[33,1024]{1,0:T(8,128)S(1)}, f32[33,1024]{1,0:T(8,128)S(1)}, u32[]{:S(2)}, u32[]{:S(2)}) collective-permute-start(f32[33,1024]{1,0:T(8,128)S(1)} %pad_maximum_fusion.own_ref), channel_id=1, source_target_pairs={{1,2},{2,1},{3,4},{4,3},{5,6},{6,5},{7,8},{8,7},{9,10},{10,9},{11,... | collective-permute-start | bytes 405512 | tf_op jit(solution)/shard_map/ppermute | solution.py:249
  26.5 0.0 collective-permute-done.1.near_ref
  26.5 4.7 %collective-permute-done.2.far_ref = f32[33,1024]{1,0:T(8,128)S(1)} collective-permute-done((f32[33,1024]{1,0:T(8,128)S(1)}, f32[33,1024]{1,0:T(8,128)S(1)}, u32[]{:S(2)}, u32[]{:S(2)}) %collective-permute-start.2) | collective-permute-done | bytes 135200 | tf_op jit(solution)/shard_map/ppermute | solution.py:249
  31.2 0.0 all-to-all-done
  31.2 0.0 copy-done
  31.2 1.6 %select.1 = (f32[256,768]{1,0:T(8,128)}, f32[16,128]{1,0:T(8,128)S(1)}) custom-call(f32[832,128]{1,0:T(8,128)S(1)} %bitcast.11, f32[8,128]{1,0:T(8,128)S(1)} %bitcast.15, f32[33,1024]{1,0:T(8,128)S(1)} %pad_maximum_fusion.own_ref, f32[33,1024]{1,0:T(8,128)S(1)} %collective-permute-done.1.near_ref, f32[33,1024]{1,0:T(8,128)S(1)} %collective-permute-done.2.far_ref), custom_call_target="tpu_custom_call" | custom-call | tf_op jit(solution)/shard_map/select/pallas_call | solution.py:122
  32.8 7.2 %all-to-all-start.1 = ((f32[8,32,768]{2,1,0:T(8,128)}), f32[8,32,768]{2,1,0:T(8,128)S(1)}, u32[]{:S(2)}, u32[]{:S(2)}) async-start(f32[8,32,768]{2,1,0:T(8,128)} %bitcast.17), calls=%async_computation.1 | async-start | bytes 1572864 | tf_op jit(solution)/shard_map/all_to_all | solution.py:252
  40.1 7.6 %collective-permute-start.3 = (f32[512,128]{1,0:T(8,128)S(1)}, f32[512,128]{1,0:T(8,128)S(1)}, u32[]{:S(2)}, u32[]{:S(2)}) collective-permute-start(f32[512,128]{1,0:T(8,128)S(1)} %bitcast.18), channel_id=1, source_target_pairs={{0,256},{256,0},{1,257},{257,1},{2,258},{258,2},{3,259},{259,3},{4... | collective-permute-start | bytes 786440 | tf_op jit(solution)/shard_map/ppermute | solution.py:256
  47.7 12.4 %collective-permute-done.3.crossed_ref = f32[512,128]{1,0:T(8,128)S(1)} collective-permute-done((f32[512,128]{1,0:T(8,128)S(1)}, f32[512,128]{1,0:T(8,128)S(1)}, u32[]{:S(2)}, u32[]{:S(2)}) %collective-permute-start.3) | collective-permute-done | bytes 262176 | tf_op jit(solution)/shard_map/ppermute | solution.py:256
  60.2 2.0 %all-to-all-done.1 = f32[8,32,768]{2,1,0:T(8,128)S(1)} async-done(((f32[8,32,768]{2,1,0:T(8,128)}), f32[8,32,768]{2,1,0:T(8,128)S(1)}, u32[]{:S(2)}, u32[]{:S(2)}) %all-to-all-start.1) | async-done | bytes 786464 | tf_op jit(solution)/shard_map/all_to_all | solution.py:252
  62.2 5.8 %analyse.1 = f32[256,256]{1,0:T(8,128)S(1)} custom-call(f32[256,768]{1,0:T(8,128)S(1)} %bitcast.13, f32[16,128]{1,0:T(8,128)S(1)} %get-tuple-element.8.scales_ref, f32[832,128]{1,0:T(8,128)S(1)} %bitcast.12, f32[512,128]{1,0:T(8,128)S(1)} %collective-permute-done.3.crossed_ref), custom_call_target="tpu_custom_call" | custom-call | tf_op jit(solution)/shard_map/analyse/pallas_call | solution.py:229
  68.0 24.6 %all_to_all.31 = f32[16,16,256]{2,1,0:T(8,128)S(1)} all-to-all(f32[16,16,256]{2,1,0:T(8,128)S(1)} %bitcast.14), channel_id=1, replica_groups=mesh['half'=2,'ring'=8,'reg'=32] {'half','ring'}, dimensions={0} | all-to-all | bytes 524288 | tf_op jit(solution)/shard_map/all_to_all | solution.py:258
  92.6 0.7 copy.7
  (2 shorter events, 0.0 us)
Async XLA Ops:
  1.8 7.7 %copy-start.1 = (f32[16,1024]{1,0:T(8,128)S(1)}, f32[16,1024]{1,0:T(8,128)}, u32[]{:S(2)}) copy-start(f32[16,1024]{1,0:T(8,128)} %obs_ref.1) | copy-start | bytes 196612
  1.8 20.7 %copy-start.2 = (f32[1024]{0:T(1024)S(1)}, f32[1024]{0:T(1024)}, u32[]{:S(2)}) copy-start(f32[1024]{0:T(1024)} %param.7) | copy-start | bytes 12292
  1.8 29.4 %all-to-all-start = ((f32[8,104,128]{2,1,0:T(8,128)}), f32[8,104,128]{2,1,0:T(8,128)S(1)}, u32[]{:S(2)}, u32[]{:S(2)}) async-start(f32[8,104,128]{2,1,0:T(8,128)} %bitcast), calls=%async_computation | async-start | bytes 851968 | tf_op jit(solution)/shard_map/all_to_all | solution.py:246
  9.5 13.0 %collective-permute-start = (f32[16,1024]{1,0:T(8,128)S(1)}, f32[16,1024]{1,0:T(8,128)S(1)}, u32[]{:S(2)}, u32[]{:S(2)}) collective-permute-start(f32[16,1024]{1,0:T(8,128)S(1)} %copy-done.1), channel_id=1, source_target_pairs={{0,256},{256,0},{1,257},{257,1},{2,258},{258,2},{3,259},{259,3},{4... | collective-permute-start | bytes 196616 | tf_op jit(solution)/shard_map/ppermute | solution.py:244
  22.5 8.7 %copy-start = (f32[1,8,128]{2,1,0:T(8,128)S(1)}, f32[1,8,128]{2,1,0:T(8,128)}, u32[]{:S(2)}) copy-start(f32[1,8,128]{2,1,0:T(8,128)} %param.9) | copy-start | bytes 12292
  22.5 3.9 %collective-permute-start.1 = (f32[33,1024]{1,0:T(8,128)S(1)}, f32[33,1024]{1,0:T(8,128)S(1)}, u32[]{:S(2)}, u32[]{:S(2)}) collective-permute-start(f32[33,1024]{1,0:T(8,128)S(1)} %pad_maximum_fusion.own_ref), channel_id=1, source_target_pairs={{0,1},{1,0},{2,3},{3,2},{4,5},{5,4},{6,7},{7,6},{8,9},{9,8},{10,11... | collective-permute-start | bytes 405512 | tf_op jit(solution)/shard_map/ppermute | solution.py:250
  24.5 6.7 %collective-permute-start.2 = (f32[33,1024]{1,0:T(8,128)S(1)}, f32[33,1024]{1,0:T(8,128)S(1)}, u32[]{:S(2)}, u32[]{:S(2)}) collective-permute-start(f32[33,1024]{1,0:T(8,128)S(1)} %pad_maximum_fusion.own_ref), channel_id=1, source_target_pairs={{1,2},{2,1},{3,4},{4,3},{5,6},{6,5},{7,8},{8,7},{9,10},{10,9},{11,... | collective-permute-start | bytes 405512 | tf_op jit(solution)/shard_map/ppermute | solution.py:249
  32.8 29.3 %all-to-all-start.1 = ((f32[8,32,768]{2,1,0:T(8,128)}), f32[8,32,768]{2,1,0:T(8,128)S(1)}, u32[]{:S(2)}, u32[]{:S(2)}) async-start(f32[8,32,768]{2,1,0:T(8,128)} %bitcast.17), calls=%async_computation.1 | async-start | bytes 1572864 | tf_op jit(solution)/shard_map/all_to_all | solution.py:252
  40.1 20.1 %collective-permute-start.3 = (f32[512,128]{1,0:T(8,128)S(1)}, f32[512,128]{1,0:T(8,128)S(1)}, u32[]{:S(2)}, u32[]{:S(2)}) collective-permute-start(f32[512,128]{1,0:T(8,128)S(1)} %bitcast.18), channel_id=1, source_target_pairs={{0,256},{256,0},{1,257},{257,1},{2,258},{258,2},{3,259},{259,3},{4... | collective-permute-start | bytes 786440 | tf_op jit(solution)/shard_map/ppermute | solution.py:256
